TPU v7x, 32 devices: a whole 2x2x4 slice. The times are simulated.
32 devices in a mesh: parts: 2 (over x), dp: 4 (over y, core), shard: 4 (over z).
Axes of the slice: x: 2, y: 2, z: 4, core: 2. Of those that a mesh axis runs over, the one named last changes fastest.
Arguments:
- projected: bfloat16 [7680, 7680], P(('parts', 'dp', 'shard')), parts along dimension 0, may hold values from -4 to 4
- residual: bfloat16 [7680, 2560], P(('parts', 'dp', 'shard')), parts along dimension 0, may hold values from -6 to 6
- out_weight: bfloat16 [2560, 2560], P(None, 'shard'), may hold values from -0.125 to 0.125
- probe_weight: bfloat16 [2, 2560, 8], replicated, may hold values from -0.125 to 0.125
- labels: int32 [7680], P(('parts', 'dp', 'shard')), parts along dimension 0, may hold values from 0 to 7
- lengths: int32 [32, 9], P(('parts', 'dp', 'shard')), parts along dimension 0, may hold values from 12 to 48, as said below
- destination: int32 [32, 9], P(('parts', 'dp', 'shard')), parts along dimension 0, may hold values from 0 to 3, as said below
Outputs:
- hidden_rows: bfloat16 [18432, 2560], P(('parts', 'dp', 'shard')), parts along dimension 0
- probe_grad: float32 [4, 2560, 8], P('parts'), parts along dimension 0
There are 2 independent parts, one for each index of `parts`. A program takes and returns all parts, laid end to end along the dimension named above; an argument that names none is the same for every part. Nothing has to cross between parts.
Inputs may be any that keep to these rules, and one draw needn't show every extreme that they name: Each row of lengths sums to 240 and holds exactly one protein of length 48. `destination`: A loader assigns at most 3 proteins to any one dp index; in every shard column one dp index is assigned exactly 3 proteins by every loader of that column.
All inputs are finite; a program needn't handle non-finite values.
Results may differ from a plain program's by a relative error of at most 0.0031.
Values may be sent and summed in bfloat16 or wider, within the bound.
No kernel may reach another device: no remote copies, remote signals or barrier semaphores. Data moves between devices by JAX's collectives and lax.ppermute only.
A program may use at most 128 MiB of HBM per device.

v0:
```python
import jax
import jax.numpy as jnp
from jax import lax
from jax.sharding import PartitionSpec as P

HS = 128
CLASSES = 8
LMAX = 48
TOK_DEV = 240


def attend(blocks, block_lengths):
    block_count = blocks.shape[0]
    span_rows = blocks.shape[1]
    head_width = blocks.shape[2] // 3
    head_count = head_width // HS
    queries = blocks[:, :, :head_width].reshape(block_count, span_rows, head_count, HS)
    key_rows = blocks[:, :, head_width : 2 * head_width].reshape(
        block_count, span_rows, head_count, HS
    )
    value_rows = blocks[:, :, 2 * head_width :].reshape(block_count, span_rows, head_count, HS)
    scores = jnp.einsum(
        "plhs,pmhs->phlm", queries, key_rows, preferred_element_type=jnp.float32
    ) * HS ** (-0.5)
    keep_mask = (jnp.arange(span_rows, dtype=jnp.int32)[None, :] < block_lengths[:, None]).astype(
        jnp.float32
    )
    weights = jnp.exp(scores) * keep_mask[:, None, None, :]
    denominator = (
        jnp.sum(weights, axis=-1, keepdims=True)
        + (block_lengths == 0).astype(jnp.float32)[:, None, None, None]
    )
    weight_low = (weights / denominator).astype(jnp.bfloat16)
    attended = jnp.einsum(
        "phlm,pmhs->plhs", weight_low, value_rows, preferred_element_type=jnp.float32
    )
    return attended.reshape(block_count * span_rows, head_width).astype(jnp.bfloat16)


def project(attended, out_weight):
    return jnp.dot(
        attended,
        lax.all_gather(out_weight, "shard", axis=1, tiled=True),
        preferred_element_type=jnp.float32,
    )


def probe_terms(represent_x, represent_h, label_rows, keep_mask, probe_weight):
    one_hot = (label_rows[:, None] == jnp.arange(CLASSES, dtype=jnp.int32)[None, :]).astype(
        jnp.float32
    )
    collected = []
    for which, represent in enumerate((represent_x, represent_h)):
        logits = jnp.dot(represent, probe_weight[which], preferred_element_type=jnp.float32)
        exponent = jnp.exp(logits)
        likelihood = exponent / jnp.sum(exponent, axis=1, keepdims=True)
        mismatch = ((likelihood - one_hot) * keep_mask[:, None] / TOK_DEV).astype(jnp.bfloat16)
        collected.append(
            lax.dot_general(
                represent, mismatch, (((0,), (0,)), ((), ())), preferred_element_type=jnp.float32
            )
        )
    return jnp.stack(collected)


def per_device(projected, residual, out_weight, probe_weight, labels, lengths, destination):
    group_size = lax.axis_size("dp")
    prot_count = lengths.shape[1]
    slot_count = -(-prot_count // group_size)
    tok_count = projected.shape[0]
    lens_own = lengths[0]
    dest_own = destination[0]
    starts = jnp.cumsum(lens_own) - lens_own
    offsets = jnp.arange(LMAX, dtype=jnp.int32)
    positions = jnp.arange(prot_count, dtype=jnp.int32)
    same_dest = dest_own[:, None] == dest_own[None, :]
    earlier = positions[:, None] > positions[None, :]
    slot_rank = jnp.sum((same_dest & earlier).astype(jnp.int32), axis=1)
    slot_match = (
        dest_own[None, None, :] == jnp.arange(group_size, dtype=jnp.int32)[:, None, None]
    ) & (slot_rank[None, None, :] == jnp.arange(slot_count, dtype=jnp.int32)[None, :, None])
    match_int = slot_match.astype(jnp.int32)
    slot_start = jnp.sum(match_int * starts, axis=2)
    slot_len = jnp.sum(match_int * lens_own, axis=2)
    block_count = group_size * slot_count
    row_index = jnp.minimum(slot_start[:, :, None] + offsets, tok_count - 1).reshape(
        group_size, slot_count * LMAX
    )
    live_rows = (offsets[None, None, :] < slot_len[:, :, None]).reshape(
        group_size, slot_count * LMAX
    )
    rows_send = jnp.where(live_rows[:, :, None], jnp.take(projected, row_index, axis=0), 0)
    resid_send = jnp.where(live_rows[:, :, None], jnp.take(residual, row_index, axis=0), 0)
    label_send = jnp.where(live_rows, jnp.take(labels, row_index), 0)
    got_labels, got_lengths = (
        lax.all_to_all(label_send, "dp", split_axis=0, concat_axis=0, tiled=True),
        lax.all_to_all(slot_len, "dp", split_axis=0, concat_axis=0, tiled=True),
    )
    got_rows, got_resid = (
        lax.all_to_all(rows_send, "dp", split_axis=0, concat_axis=0, tiled=True),
        lax.all_to_all(resid_send, "dp", split_axis=0, concat_axis=0, tiled=True),
    )
    lengths_recv = got_lengths.reshape(block_count)
    attended = attend(got_rows.reshape(block_count, LMAX, -1), lengths_recv)
    keep_mask = (offsets[None, :] < lengths_recv[:, None]).astype(jnp.float32).reshape(-1)
    represent = got_resid.reshape(block_count * LMAX, -1)
    mixed_rows = project(attended, out_weight) + represent.astype(jnp.float32)
    hidden = (mixed_rows * keep_mask[:, None]).astype(jnp.bfloat16)
    grad_terms = probe_terms(represent, hidden, got_labels.reshape(-1), keep_mask, probe_weight)
    grad_sum = lax.psum(grad_terms, ("dp", "shard"))
    return (hidden, grad_sum)


def solution(mesh):
    return jax.shard_map(
        per_device,
        mesh=mesh,
        in_specs=(
            P(("parts", "dp", "shard"), None),
            P(("parts", "dp", "shard"), None),
            P(None, "shard"),
            P(),
            P(("parts", "dp", "shard")),
            P(("parts", "dp", "shard"), None),
            P(("parts", "dp", "shard"), None),
        ),
        out_specs=(P(("parts", "dp", "shard"), None), P("parts", None, None)),
        check_vma=False,
    )
```

profile of v0, /device:TPU:8, one launch (start us, length us, event | category | flops | bytes accessed | tf_op | source)
XLA Modules:
  0.0 349.7 jit_solution(5877579920904036037)
XLA Ops:
  7.2 0.7 all-gather.2.cloned.1.call-update
  8.3 0.2 fusion.37
  8.5 0.7 copy.27
  9.2 3.2 all-to-all-start.1
  13.4 4.2 %gather_fusion.1 = bf16[576,2560]{1,0:T(8,128)(2,1)} fusion(bf16[240,2560]{1,0:T(8,128)(2,1)S(1)} %copy-done, s32[1024]{0:T(1024)S(1)} %pad_clamp_fusion), kind=kCustom, calls=%fused_computation.1 | custom fusion | bytes 5900544 | tf_op jit(solution)/shard_map/jit(_take)/gather | solution.py:93
  17.6 3.9 %gather_fusion.2 = s32[576]{0:T(1024)S(1)} fusion(s32[240]{0:T(256)S(1)} %copy-done.2, s32[1024]{0:T(1024)S(1)} %pad_clamp_fusion), kind=kCustom, calls=%fused_computation.2 | custom fusion | bytes 6912 | tf_op jit(solution)/shard_map/jit(_take)/gather | solution.py:94
  21.6 0.6 copy.31
  22.3 3.3 all-to-all-start.3
  25.5 4.2 %select_select_fusion.1 = bf16[4,144,2560]{2,1,0:T(8,128)(2,1)} fusion(bf16[4,144,2560]{2,1,0:T(8,128)(2,1)} %bitcast.61, pred[4,144]{1,0:T(4,128)(4,1)S(1)} %get-tuple-element.8, pred[4,144]{1,0:T(4,128)(4,1)S(1)} %get-tuple-element.7), kind=kLoop, calls=%fused_computation.23 | loop fusion | flops 2949120 | bytes 5899392 | tf_op jit(solution)/shard_map/jit(_where)/select_n | solution.py:93
  29.7 22.4 %gather_fusion = bf16[576,7680]{1,0:T(8,128)(2,1)} fusion(bf16[240,7680]{1,0:T(8,128)(2,1)} %param.7, s32[1024]{0:T(1024)S(1)} %pad_clamp_fusion), kind=kCustom, calls=%fused_computation | custom fusion | bytes 17697024 | tf_op jit(solution)/shard_map/jit(_take)/gather | solution.py:92
  52.1 4.6 %all-to-all-start.2 = ((bf16[4,144,2560]{2,1,0:T(8,128)(2,1)}), bf16[4,144,2560]{2,1,0:T(8,128)(2,1)}, u32[]{:S(2)}, u32[]{:S(2)}) async-start(bf16[4,144,2560]{2,1,0:T(8,128)(2,1)} %select_select_fusion.1), calls=%async_computation.2 | async-start | bytes 5898240 | tf_op jit(solution)/shard_map/all_to_all | solution.py:101
  56.8 8.1 %select_select_fusion = bf16[4,144,7680]{2,1,0:T(8,128)(2,1)} fusion(bf16[4,144,7680]{2,1,0:T(8,128)(2,1)} %bitcast.60, pred[4,144]{1,0:T(4,128)(4,1)S(1)} %get-tuple-element.8, pred[4,144]{1,0:T(4,128)(4,1)S(1)} %get-tuple-element.7), kind=kLoop, calls=%fused_computation.3 | loop fusion | flops 8847360 | bytes 17695872 | tf_op jit(solution)/shard_map/jit(_where)/select_n | solution.py:92
  64.9 26.7 %all-to-all-done.2 = bf16[4,144,2560]{2,1,0:T(8,128)(2,1)} async-done(((bf16[4,144,2560]{2,1,0:T(8,128)(2,1)}), bf16[4,144,2560]{2,1,0:T(8,128)(2,1)}, u32[]{:S(2)}, u32[]{:S(2)}) %all-to-all-start.2) | async-done | bytes 2949152 | tf_op jit(solution)/shard_map/all_to_all | solution.py:101
  91.6 5.7 %all-to-all-start = ((bf16[4,144,7680]{2,1,0:T(8,128)(2,1)}), bf16[4,144,7680]{2,1,0:T(8,128)(2,1)}, u32[]{:S(2)}, u32[]{:S(2)}) async-start(bf16[4,144,7680]{2,1,0:T(8,128)(2,1)} %select_select_fusion), calls=%async_computation | async-start | bytes 17694720 | tf_op jit(solution)/shard_map/all_to_all | solution.py:100
  97.3 0.2 all-reduce.2.cloned.1.call-start
  97.5 0.5 broadcast.237
  98.1 0.7 reduce.4
  99.1 2.7 fusion.43
  101.8 2.3 convolution_bitcast_fusion.1
  104.1 91.3 %all-to-all-done = bf16[4,144,7680]{2,1,0:T(8,128)(2,1)} async-done(((bf16[4,144,7680]{2,1,0:T(8,128)(2,1)}), bf16[4,144,7680]{2,1,0:T(8,128)(2,1)}, u32[]{:S(2)}, u32[]{:S(2)}) %all-to-all-start) | async-done | bytes 8847392 | tf_op jit(solution)/shard_map/all_to_all | solution.py:100
  195.4 4.0 %slice_bitcast_fusion.2 = (bf16[12,6,20,8,128]{4,3,2,1,0:T(8,128)(2,1)S(1)}, bf16[12,6,20,8,128]{4,3,2,1,0:T(8,128)(2,1)S(1)}, bf16[12,6,20,8,128]{4,3,2,1,0:T(8,128)(2,1)S(1)}) fusion(bf16[12,48,7680]{2,1,0:T(8,128)(2,1)} %bitcast.5), kind=kLoop, calls=%fused_computation.22 | loop fusion | bytes 17694720
  199.4 1.7 fusion
  201.2 2.0 convert_bitcast_fusion
  203.2 2.6 copy.30
  205.8 28.8 %all-gather.2.cloned.1.call-done = bf16[2560,2560]{1,0:T(8,128)(2,1)} async-done(((bf16[2560,640]{1,0:T(8,128)(2,1)}), bf16[2560,2560]{1,0:T(8,128)(2,1)}) %all-gather.2.cloned.1.call-update) | async-done | bytes 13107216 | tf_op jit(solution)/shard_map/all_gather | solution.py:43
  234.6 12.4 %multiply_convert_fusion = bf16[576,2560]{1,0:T(8,128)(2,1)S(1)} fusion(bf16[576,2560]{1,0:T(8,128)(2,1)} %bitcast.9, bf16[2560,2560]{1,0:T(8,128)(2,1)} %all-gather.2.cloned.1.call-done, bf16[72,8,20,128]{3,2,1,0:T(8,128)(2,1)} %bitcast.62, f32[576]{0:T(1024)S(1)} %reshape.360), kind=kOutput, calls=%fused_computation.4 | convolution fusion | flops 7555645440 | bytes 21956864 | tf_op jit(solution)/shard_map/dot_general | solution.py:41
  246.9 0.9 fusion.42
  247.8 0.5 convolution_bitcast_fusion
  248.3 0.2 copy-done.3
  248.5 0.7 pad_maximum_fusion
  249.2 92.1 %all-reduce.2.cloned.1.call-done = f32[2,2560,8]{1,2,0:T(8,128)} async-done(((f32[2,2560,8]{1,2,0:T(8,128)}), f32[2,2560,8]{1,2,0:T(8,128)}) %all-reduce.2.cloned.1.call-update) | async-done | bytes 163856 | tf_op jit(solution)/shard_map/psum | solution.py:110
  341.3 1.6 copy.62
  (46 shorter events, 1.9 us)
Async XLA Ops:
  7.2 6.2 %copy-start = (bf16[240,2560]{1,0:T(8,128)(2,1)S(1)}, bf16[240,2560]{1,0:T(8,128)(2,1)}, u32[]{:S(2)}) copy-start(bf16[240,2560]{1,0:T(8,128)(2,1)} %param.8) | copy-start | bytes 3686404
  7.2 0.8 copy-start.5
  7.2 0.9 copy-start.6
  7.2 227.4 %all-gather.2.cloned.1.call-start = ((), (), s32[]{:S(2)}) async-start(), calls=%async_computation.4 | async-start | bytes 16384000 | tf_op jit(solution)/shard_map/all_gather | solution.py:43
  9.2 13.1 %all-to-all-start.1 = ((s32[4,1,3]{2,1,0:T(1,128)}), s32[4,1,3]{2,1,0:T(1,128)S(1)}, u32[]{:S(2)}, u32[]{:S(2)}) async-start(s32[4,1,3]{2,1,0:T(1,128)} %copy.27), calls=%async_computation.1 | async-start | bytes 4096 | tf_op jit(solution)/shard_map/all_to_all | solution.py:97
  13.4 4.2 %copy-start.2 = (s32[240]{0:T(256)S(1)}, s32[240]{0:T(256)}, u32[]{:S(2)}) copy-start(s32[240]{0:T(256)} %param.11) | copy-start | bytes 2884
  22.3 29.9 %all-to-all-start.3 = ((s32[4,1,144]{2,1,0:T(1,128)}), s32[4,1,144]{2,1,0:T(1,128)S(1)}, u32[]{:S(2)}, u32[]{:S(2)}) async-start(s32[4,1,144]{2,1,0:T(1,128)} %copy.31), calls=%async_computation.3 | async-start | bytes 8192 | tf_op jit(solution)/shard_map/all_to_all | solution.py:96
  52.1 39.5 %all-to-all-start.2 = ((bf16[4,144,2560]{2,1,0:T(8,128)(2,1)}), bf16[4,144,2560]{2,1,0:T(8,128)(2,1)}, u32[]{:S(2)}, u32[]{:S(2)}) async-start(bf16[4,144,2560]{2,1,0:T(8,128)(2,1)} %select_select_fusion.1), calls=%async_computation.2 | async-start | bytes 5898240 | tf_op jit(solution)/shard_map/all_to_all | solution.py:101
  64.9 34.2 %copy-start.4 = (bf16[2,2560,8]{1,2,0:T(8,128)(2,1)S(1)}, bf16[2,2560,8]{1,2,0:T(8,128)(2,1)}, u32[]{:S(2)}) copy-start(bf16[2,2560,8]{1,2,0:T(8,128)(2,1)} %param.10) | copy-start | bytes 245764
  91.6 103.8 %all-to-all-start = ((bf16[4,144,7680]{2,1,0:T(8,128)(2,1)}), bf16[4,144,7680]{2,1,0:T(8,128)(2,1)}, u32[]{:S(2)}, u32[]{:S(2)}) async-start(bf16[4,144,7680]{2,1,0:T(8,128)(2,1)} %select_select_fusion), calls=%async_computation | async-start | bytes 17694720 | tf_op jit(solution)/shard_map/all_to_all | solution.py:100
  97.3 244.0 %all-reduce.2.cloned.1.call-start = ((), (), s32[]{:S(2)}) async-start(), calls=%async_computation.5 | async-start | bytes 327680 | tf_op jit(solution)/shard_map/psum | solution.py:110
  246.9 1.6 copy-start.3
  247.8 95.1 %copy-start.1 = (bf16[240,2560]{1,0:T(8,128)(2,1)S(1)}, bf16[240,2560]{1,0:T(8,128)(2,1)}, u32[]{:S(2)}) copy-start(bf16[240,2560]{1,0:T(8,128)(2,1)} %param.8) | copy-start | bytes 3686404
Sparse Core Ops, SparseCore 0:
  9.6 224.9 all-gather.1
  249.4 91.8 all-reduce.1
where the time goes:
time: 350 us
  waiting for transfers between devices  240 us (69%)
  local copies, waits for them, and re-layouts  42 us (12%)
  matrix products  22.5 us (6%)
  starting transfers between devices  17 us (5%)
  other arithmetic  14.4 us (4%)
  between operations  14.3 us (4%)
    psum x1, waiting for transfers between devices, per_device(): grad_sum = lax.psum(grad_terms, ('dp', 'shard'))  92.1 us
    all_to_all x1, waiting for transfers between devices, per_device(): lax.all_to_all(rows_send, 'dp', split_axis=0, concat_axis=0, tiled=True)  91.3 us
    all_gather x1, waiting for transfers between devices, project(): lax.all_gather(out_weight, 'shard', axis=1, tiled=True)  28.8 us
    all_to_all x1, waiting for transfers between devices, per_device(): lax.all_to_all(resid_send, 'dp', split_axis=0, concat_axis=0, tiled=True)  26.7 us
    gather x1, local copies, waits for them, and re-layouts, per_device(): jnp.take(projected, row_index, axis=0)  22.4 us
    dot_general x1, matrix products, project(): jnp.dot(attended, lax.all_gather(out_weight, 'shard', axis=1, tiled=True)...  12.4 us
    select_n x1, other arithmetic, per_device(): jnp.where(live_rows[:, :, None], jnp.take(projected, row_index, axis=0), 0)  8.14 us
  transfers between devices with their start and end apart: 6, of which 4 were waited for; matrix products, arithmetic and copies ran while one was open for 18% of the time, Pallas kernels for 0%

commit v1 on v0

v1 whole, which is shorter than its diff:
```python
import functools

import jax
import jax.numpy as jnp
from jax import lax
from jax.experimental import pallas as pl
from jax.experimental.pallas import tpu as pltpu
from jax.sharding import PartitionSpec as P

HS = 128
CLASSES = 8
LMAX = 48
LANES = 128

VMEM = pl.BlockSpec(memory_space=pltpu.VMEM)
SMEM = pl.BlockSpec(memory_space=pltpu.SMEM)
ANY = pl.BlockSpec(memory_space=pl.ANY)


def is_pow2(n):
    return n & (n - 1) == 0


def aligned(value, unit):
    return pl.multiple_of(value, unit)


def attention_kernel(
    prot_count, slot_count, group, len_ref, dest_ref, me_ref, q_ref, k_ref, v_ref, att_ref, sel_ref, mask_ref
):
    rows = q_ref.shape[0]

    @pl.when(pl.program_id(0) == 0)
    def _():
        starts = []
        total = 0
        for p in range(prot_count):
            starts.append(total)
            total = total + len_ref[p]
        row = lax.broadcasted_iota(jnp.int32, (rows, rows), 0)
        col = lax.broadcasted_iota(jnp.int32, (rows, rows), 1)
        row_low, row_high = jnp.zeros_like(row), jnp.zeros_like(row)
        for p in range(prot_count):
            inside = (row >= starts[p]) & (row < starts[p] + len_ref[p])
            row_low = jnp.where(inside, starts[p], row_low)
            row_high = jnp.where(inside, starts[p] + len_ref[p], row_high)
        mask_ref[...] = ((col >= row_low) & (col < row_high)).astype(jnp.float32)

        ranks = []
        for p in range(prot_count):
            rank = 0
            for q in range(p):
                rank = rank + (dest_ref[q] == dest_ref[p]).astype(jnp.int32)
            ranks.append(rank)
        t_row = lax.broadcasted_iota(jnp.int32, (LMAX, rows), 0)
        t_col = lax.broadcasted_iota(jnp.int32, (LMAX, rows), 1)
        me = me_ref[0]
        for j in range(group):
            target = peer(me, j, group)
            for r in range(slot_count):
                start, length = jnp.int32(0), jnp.int32(0)
                for p in range(prot_count):
                    hit = (dest_ref[p] == target) & (ranks[p] == r)
                    start = jnp.where(hit, starts[p], start)
                    length = jnp.where(hit, len_ref[p], length)
                chosen = (t_col == t_row + start) & (t_row < length)
                block = (j * slot_count + r) * LMAX
                sel_ref[block : block + LMAX, :] = chosen.astype(jnp.float32).astype(jnp.bfloat16)

    for h in range(q_ref.shape[1] // HS):
        cols = slice(h * HS, (h + 1) * HS)
        scores = lax.dot_general(
            q_ref[:, cols], k_ref[:, cols], (((1,), (1,)), ((), ())), preferred_element_type=jnp.float32
        ) * HS ** (-0.5)
        weights = jnp.where(mask_ref[...] > 0, jnp.exp(scores), 0.0)
        total = jnp.sum(weights, axis=1, keepdims=True)
        low = (weights / total).astype(jnp.bfloat16)
        att_ref[:, cols] = jnp.dot(low, v_ref[:, cols], preferred_element_type=jnp.float32).astype(jnp.bfloat16)


def attention(projected, lengths, destination, me, group, slot_count):
    rows, width = projected.shape
    hidden = width // 3
    per = 4 * HS if hidden % (4 * HS) == 0 else HS
    steps = hidden // per
    prot_count = lengths.shape[0]
    sel_rows = group * slot_count * LMAX
    return pl.pallas_call(
        functools.partial(attention_kernel, prot_count, slot_count, group),
        grid_spec=pltpu.PrefetchScalarGridSpec(
            num_scalar_prefetch=3,
            grid=(steps,),
            in_specs=[
                pl.BlockSpec((rows, per), lambda i, *_: (0, i)),
                pl.BlockSpec((rows, per), lambda i, *_: (0, i + steps)),
                pl.BlockSpec((rows, per), lambda i, *_: (0, i + 2 * steps)),
            ],
            out_specs=[
                pl.BlockSpec((rows, per), lambda i, *_: (0, i)),
                pl.BlockSpec((sel_rows, rows), lambda i, *_: (0, 0)),
            ],
            scratch_shapes=[pltpu.VMEM((rows, rows), jnp.float32)],
        ),
        out_shape=[
            jax.ShapeDtypeStruct((rows, hidden), jnp.bfloat16),
            jax.ShapeDtypeStruct((sel_rows, rows), jnp.bfloat16),
        ],
        name="attention",
    )(lengths, destination, me, projected, projected, projected)


def project_kernel(piece_count, group, where_ref, att_ref, resid_ref, sel_ref, *refs):
    pieces, (hid_ref, *send_refs) = refs[:piece_count], refs[piece_count:]
    width = hid_ref.shape[1]
    total = None
    for i, piece in enumerate(pieces):
        depth = piece.shape[0]
        if piece_count == 1:
            rows = att_ref[...]
        else:
            rows = att_ref[:, pl.ds(aligned(where_ref[1 + i], LANES), depth)]
        part = jnp.dot(rows, piece[...], preferred_element_type=jnp.float32)
        total = part if total is None else total + part
    if resid_ref.shape[1] == width:
        resid = resid_ref[...]
    else:
        resid = resid_ref[:, pl.ds(aligned(where_ref[0], LANES), width)]
    hid_ref[...] = (total + resid.astype(jnp.float32)).astype(jnp.bfloat16)
    span = sel_ref.shape[0] // group
    for j, send in enumerate(send_refs):
        send[...] = jnp.dot(
            sel_ref[j * span : (j + 1) * span, :], hid_ref[...], preferred_element_type=jnp.float32
        ).astype(jnp.bfloat16)


def project(where, att, resid, sel, pieces, group):
    rows, width = att.shape[0], pieces[0].shape[1]
    span = sel.shape[0] // group
    return pl.pallas_call(
        functools.partial(project_kernel, len(pieces), group),
        in_specs=[SMEM] + [VMEM] * (3 + len(pieces)),
        out_specs=[VMEM] * (1 + group),
        out_shape=[jax.ShapeDtypeStruct((rows, width), jnp.bfloat16)]
        + [jax.ShapeDtypeStruct((span, width), jnp.bfloat16)] * group,
        name="project",
    )(where, att, resid, sel, *pieces)


def probe_kernel(chunk_widths, tok_count, where_ref, label_ref, probe_ref, *refs):
    chunks, grad_ref = refs[: len(chunk_widths)], refs[len(chunk_widths)]
    logits = None
    for i, chunk in enumerate(chunks):
        cols = pl.ds(aligned(where_ref[i], LANES), chunk_widths[i]) if len(chunks) > 1 else slice(None)
        part = lax.dot_general(
            probe_ref[:, cols], chunk[...], (((1,), (1,)), ((), ())), preferred_element_type=jnp.float32
        )
        logits = part if logits is None else logits + part
    exponent = jnp.exp(logits)
    likelihood = exponent / jnp.sum(exponent, axis=0, keepdims=True)
    one_hot = (lax.broadcasted_iota(jnp.int32, logits.shape, 0) == label_ref[...]).astype(jnp.float32)
    mismatch = ((likelihood - one_hot) / tok_count).astype(jnp.bfloat16)
    for i, chunk in enumerate(chunks):
        cols = pl.ds(aligned(where_ref[i], LANES), chunk_widths[i]) if len(chunks) > 1 else slice(None)
        grad_ref[:, cols] = jnp.dot(mismatch, chunk[...], preferred_element_type=jnp.float32)


def probe_grad(where, labels, probe, chunks):
    tok_count = labels.shape[1]
    return pl.pallas_call(
        functools.partial(probe_kernel, tuple(c.shape[1] for c in chunks), tok_count),
        in_specs=[SMEM] + [VMEM] * (2 + len(chunks)),
        out_specs=VMEM,
        out_shape=jax.ShapeDtypeStruct(probe.shape, jnp.float32),
        name="probe",
    )(where, labels, probe, *chunks)


def place_kernel(count, width, where_ref, *refs):
    out_ref, sems = refs[-2], refs[-1]
    copies = []
    for j in range(count):
        span = refs[j].shape[0]
        copies.append(
            pltpu.make_async_copy(
                refs[j],
                out_ref.at[
                    pl.ds(aligned(where_ref[1 + j] * span, 16), span),
                    pl.ds(aligned(where_ref[0], LANES), width),
                ],
                sems.at[j],
            )
        )
    for copy in copies:
        copy.start()
    for copy in copies:
        copy.wait()


def place(where, blocks, out, shape):
    count, width = len(blocks), blocks[0].shape[1]
    held = [] if out is None else [out]
    return pl.pallas_call(
        functools.partial(place_kernel, count, width),
        in_specs=[SMEM] + [ANY] * (count + len(held)),
        out_specs=ANY,
        out_shape=jax.ShapeDtypeStruct(shape, jnp.bfloat16),
        scratch_shapes=[pltpu.SemaphoreType.DMA((count,))],
        input_output_aliases={1 + count: 0} if held else {},
        name="place",
    )(where, *blocks, *held)


def peer(me, j, n):
    return me ^ j if is_pow2(n) else lax.rem(me + j, n)


def source(me, j, n):
    return me ^ j if is_pow2(n) else lax.rem(me + n - j, n)


def swap(x, axis, j):
    n = lax.axis_size(axis)
    return lax.ppermute(x, axis, [(i, int(i ^ j) if is_pow2(n) else (i + j) % n) for i in range(n)])


def tree_sum(terms):
    while len(terms) > 1:
        terms = [a + b for a, b in zip(terms[::2], terms[1::2])]
    return terms[0]


def sum_over_group(x, me):
    group, ring = lax.axis_size("dp"), lax.axis_size("shard")
    piece = x.shape[1] // group
    if group > 4 or not (is_pow2(group) and is_pow2(ring)) or x.shape[1] % group:
        return lax.psum(x, ("dp", "shard"))

    def cut(j):
        return lax.dynamic_slice(x, (0, (me ^ j) * piece), (x.shape[0], piece))

    mine = tree_sum([cut(0)] + [swap(cut(j), "dp", j) for j in range(1, group)])
    mine = tree_sum([mine] + [swap(mine, "shard", j) for j in range(1, ring)])
    total = jnp.zeros_like(x)
    for j in range(group):
        part = swap(mine, "dp", j) if j else mine
        total = lax.dynamic_update_slice(total, part, (0, (me ^ j) * piece))
    return total


def per_device(projected, residual, out_weight, probe_weight, labels, lengths, destination):
    group, ring, parts = lax.axis_size("dp"), lax.axis_size("shard"), lax.axis_size("parts")
    me = lax.axis_index("dp").astype(jnp.int32)
    z = lax.axis_index("shard").astype(jnp.int32)
    x = lax.axis_index("parts").astype(jnp.int32)
    slot_count = -(-lengths.shape[1] // group)
    inner, columns = out_weight.shape
    hidden_width = residual.shape[1]
    rows_out = group * slot_count * LMAX

    cores = 2 if group > 1 and is_pow2(group) else 1
    pairs = 2 if parts == 2 else 1
    shares = pairs * cores
    depth = inner // shares
    mine = (x % pairs) * cores + me % cores
    easy = columns % LANES == 0 and depth % LANES == 0
    splits = SPLITS if easy and sum(SPLITS) == columns else (columns,)

    ring_next = [(i, (i + 1) % ring) for i in range(ring)]
    offsets = [sum(splits[:i]) for i in range(len(splits))]
    held = [
        lax.dynamic_slice(out_weight, (mine * depth, off), (depth, width))
        for off, width in zip(offsets, splits)
    ]

    own_scalar = me.reshape(1)
    att, sel = attention(projected, lengths[0], destination[0], own_scalar, group, slot_count)
    label_row = labels.reshape(1, -1)
    probes = jnp.swapaxes(probe_weight, 1, 2)
    zero = jnp.zeros((1,), jnp.int32)
    grad_first = sum_over_group(probe_grad(zero, label_row, probes[0], [residual]), me)

    out = None
    hidden_chunks, hidden_where = [], []

    def finish(step, off, pieces, piece_rows, out):
        width = pieces[0].shape[1]
        col = lax.rem(z + ring - step, ring) * columns + off
        resid = residual if easy else lax.dynamic_slice(residual, (0, col), (residual.shape[0], width))
        where = jnp.stack([col] + [r * depth for r in piece_rows])
        hid, *sends = project(where, att, resid, sel, pieces, group)
        hidden_chunks.append(hid)
        hidden_where.append(col)
        if group <= 4:
            blocks = [sends[0]] + [swap(s, "dp", j) for j, s in enumerate(sends) if j]
        else:
            packed = jnp.stack(sends)
            order = jnp.stack([peer(me, j, group) for j in range(group)])
            packed = jnp.zeros_like(packed).at[order].set(packed)
            packed = lax.all_to_all(packed, "dp", split_axis=0, concat_axis=0, tiled=True)
            blocks = [packed[source(me, j, group)] for j in range(group)]
        if easy:
            spots = jnp.stack([col] + [source(me, j, group) for j in range(group)])
            return place(spots, blocks, out, (rows_out, hidden_width))
        if out is None:
            out = jnp.zeros((rows_out, hidden_width), jnp.bfloat16)
        for j, block in enumerate(blocks):
            out = lax.dynamic_update_slice(out, block, (source(me, j, group) * block.shape[0], col))
        return out

    out = finish(0, 0, [out_weight], [jnp.int32(0)], out)
    for step in range(1, ring):
        for i, off in enumerate(offsets):
            held[i] = lax.ppermute(held[i], "shard", ring_next)
            pieces, piece_rows = [held[i]], [mine]
            if pairs == 2:
                pieces.append(lax.ppermute(held[i], "parts", [(0, 1), (1, 0)]))
                piece_rows.append(mine ^ cores)
            if cores == 2:
                pieces += [swap(p, "dp", 1) for p in list(pieces)]
                piece_rows += [r ^ 1 for r in piece_rows]
            out = finish(step, off, pieces, piece_rows, out)
    if easy:
        grad_second = probe_grad(jnp.stack(hidden_where), label_row, probes[1], hidden_chunks)
    else:
        full = jnp.zeros((residual.shape[0], hidden_width), jnp.bfloat16)
        for col, chunk in zip(hidden_where, hidden_chunks):
            full = lax.dynamic_update_slice(full, chunk, (0, col))
        grad_second = probe_grad(zero, label_row, probes[1], [full])
    grad_second = sum_over_group(grad_second, me)
    return out, jnp.swapaxes(jnp.stack([grad_first, grad_second]), 1, 2)


SPLITS = (384, 256)


def solution(mesh):
    return jax.shard_map(
        per_device,
        mesh=mesh,
        in_specs=(
            P(("parts", "dp", "shard"), None),
            P(("parts", "dp", "shard"), None),
            P(None, "shard"),
            P(),
            P(("parts", "dp", "shard")),
            P(("parts", "dp", "shard"), None),
            P(("parts", "dp", "shard"), None),
        ),
        out_specs=(P(("parts", "dp", "shard"), None), P("parts", None, None)),
        check_vma=False,
    )
```

time: 350 us -> 305 us (0.87); the launches traced: 350 us -> 301 us
  waiting for transfers between devices: 240 us -> 84.7 us
  Pallas kernels: 0 us -> 146 us
  starting transfers between devices: 17 us -> 49.7 us
  local copies, waits for them, and re-layouts: 42 us -> 17 us
  matrix products: 22.5 us -> 0 us
  between operations: 14.3 us -> 1.55 us
  other arithmetic: 14.4 us -> 2.75 us
    pallas_call x0 -> x17, Pallas kernels: none -> 146 us  [the longest x7 102 us: place(): pl.pallas_call(functools.partial(place_kernel, count, width), in_specs=[S...]
    all_to_all x4 -> x0, waiting for transfers between devices: 118 us -> none  [the longest x1 91.3 us: per_device(): lax.all_to_all(rows_send, 'dp', split_axis=0, concat_axis=0, tiled=True)]
    psum x1 -> x0, waiting for transfers between devices: 92.1 us -> none  [per_device(): grad_sum = lax.psum(grad_terms, ('dp', 'shard'))]
    ppermute x0 -> x63, waiting for transfers between devices: none -> 84.7 us  [the longest x6 33.9 us: per_device(): pieces.append(lax.ppermute(held[i], 'parts', [(0, 1), (1, 0)]))]
    ppermute x0 -> x63, starting transfers between devices: none -> 49.7 us  [the longest x51 34.3 us: swap(): lax.ppermute(x, axis, [(i, int(i ^ j) if is_pow2(n) else (i + j) % n) for...]
    gather x4 -> x0, local copies, waits for them, and re-layouts: 30.7 us -> none  [the longest x1 22.4 us: per_device(): jnp.take(projected, row_index, axis=0)]
    all_gather x1 -> x0, waiting for transfers between devices: 28.8 us -> none  [project(): lax.all_gather(out_weight, 'shard', axis=1, tiled=True)]
    dot_general x7 -> x0, matrix products: 22.5 us -> none  [the longest x1 12.4 us: project(): jnp.dot(attended, lax.all_gather(out_weight, 'shard', axis=1, tiled=True)...]
  transfers between devices with their start and end apart: 6 -> 63, of which waited for: 4 -> 20; matrix products, arithmetic and copies ran while one was open for 18% -> 5% of each run, Pallas kernels for 0% -> 45%
where the time goes in v1:
time: 305 us; the launch traced here: 301 us
  Pallas kernels  146 us (48%)
  waiting for transfers between devices  84.7 us (28%)
  starting transfers between devices  49.7 us (16%)
  local copies, waits for them, and re-layouts  17 us (6%)
    pallas_call x7, Pallas kernels, place(): pl.pallas_call(functools.partial(place_kernel, count, width), in_specs=[S...  102 us
    ppermute x51, starting transfers between devices, swap(): lax.ppermute(x, axis, [(i, int(i ^ j) if is_pow2(n) else (i + j) % n) for...  34.3 us
    ppermute x6, waiting for transfers between devices, per_device(): pieces.append(lax.ppermute(held[i], 'parts', [(0, 1), (1, 0)]))  33.9 us
    ppermute x51, waiting for transfers between devices, swap(): lax.ppermute(x, axis, [(i, int(i ^ j) if is_pow2(n) else (i + j) % n) for...  32.8 us
    pallas_call x7, Pallas kernels, project(): pl.pallas_call(functools.partial(project_kernel, len(pieces), group), in_...  28.8 us
    ppermute x6, waiting for transfers between devices, per_device(): held[i] = lax.ppermute(held[i], 'shard', ring_next)  18 us
    ppermute x6, starting transfers between devices, per_device(): held[i] = lax.ppermute(held[i], 'shard', ring_next)  8.56 us
    pallas_call x1, Pallas kernels, attention(): pl.pallas_call(functools.partial(attention_kernel, prot_count, slot_count...  8.21 us
  transfers between devices with their start and end apart: 63, of which 20 were waited for; matrix products, arithmetic and copies ran while one was open for 5% of the time, Pallas kernels for 45%

profile of v1, /device:TPU:8, one launch (start us, length us, event | category | flops | bytes accessed | tf_op | source)
XLA Modules:
  0.0 301.2 jit_solution(3870154652336643734)
XLA Ops:
  7.4 3.0 probe.2
  10.4 11.3 %collective-permute-done.refs_0_ = bf16[640,256]{1,0:T(8,128)(2,1)S(1)} collective-permute-done((bf16[640,256]{1,0:T(8,128)(2,1)S(1)}, bf16[640,256]{1,0:T(8,128)(2,1)S(1)}, u32[]{:S(2)}, u32[]{:S(2)}) %collective-permute-start) | collective-permute-done | bytes 327712 | tf_op jit(solution)/shard_map/ppermute | solution.py:313
  31.7 3.1 %collective-permute-start.49 = (f32[8,640]{1,0:T(8,128)S(1)}, f32[8,640]{1,0:T(8,128)S(1)}, u32[]{:S(2)}, u32[]{:S(2)}) collective-permute-start(f32[8,640]{1,0:T(8,128)S(1)} %add_add_fusion.3), channel_id=1, source_target_pairs={{0,2},{1,3},{2,0},{3,1},{4,6},{5,7},{6,4},{7,5},{8,10},{9,11},{10,... | collective-permute-start | bytes 61448 | tf_op jit(solution)/shard_map/ppermute | solution.py:223
  34.8 7.6 %collective-permute-done.48 = f32[8,640]{1,0:T(8,128)S(1)} collective-permute-done((f32[8,640]{1,0:T(8,128)S(1)}, f32[8,640]{1,0:T(8,128)S(1)}, u32[]{:S(2)}, u32[]{:S(2)}) %collective-permute-start.48) | collective-permute-done | bytes 20512 | tf_op jit(solution)/shard_map/ppermute | solution.py:223
  42.4 2.7 collective-permute-start.50
  48.7 2.1 collective-permute-start.11
  50.8 8.4 %collective-permute-done.36.refs_1_ = bf16[640,384]{1,0:T(8,128)(2,1)S(1)} collective-permute-done((bf16[640,384]{1,0:T(8,128)(2,1)S(1)}, bf16[640,384]{1,0:T(8,128)(2,1)S(1)}, u32[]{:S(2)}, u32[]{:S(2)}) %collective-permute-start.36) | collective-permute-done | bytes 491552 | tf_op jit(solution)/shard_map/ppermute | solution.py:316
  59.3 3.7 %collective-permute-done.18.refs_1_ = bf16[640,256]{1,0:T(8,128)(2,1)S(1)} collective-permute-done((bf16[640,256]{1,0:T(8,128)(2,1)}, bf16[640,256]{1,0:T(8,128)(2,1)S(1)}, u32[]{:S(2)}, u32[]{:S(2)}) %collective-permute-start.18) | collective-permute-done | bytes 327712 | tf_op jit(solution)/shard_map/ppermute | solution.py:316
  66.4 5.4 %collective-permute-done.2.refs_0_ = bf16[640,256]{1,0:T(8,128)(2,1)S(1)} collective-permute-done((bf16[640,256]{1,0:T(8,128)(2,1)}, bf16[640,256]{1,0:T(8,128)(2,1)S(1)}, u32[]{:S(2)}, u32[]{:S(2)}) %collective-permute-start.2) | collective-permute-done | bytes 327712 | tf_op jit(solution)/shard_map/ppermute | solution.py:313
  72.5 21.7 %collective-permute-done.3.refs_1_ = bf16[640,256]{1,0:T(8,128)(2,1)S(1)} collective-permute-done((bf16[640,256]{1,0:T(8,128)(2,1)S(1)}, bf16[640,256]{1,0:T(8,128)(2,1)S(1)}, u32[]{:S(2)}, u32[]{:S(2)}) %collective-permute-start.3) | collective-permute-done | bytes 327712 | tf_op jit(solution)/shard_map/ppermute | solution.py:316
  104.4 8.2 %attention.1 = (bf16[240,2560]{1,0:T(8,128)(2,1)}, bf16[576,240]{1,0:T(8,128)(2,1)}) custom-call(s32[9]{0:T(128)} %bitcast.44, s32[9]{0:T(128)} %bitcast.45, s32[1]{0:T(128)} %bitcast.1.me_ref, bf16[240,7680]{1,0:T(8,128)(2,1)} %v_ref.1, bf16[240,7680]{1,0:T(8,128)(2,1)} %v_ref.1, bf16[240,7680]{1,0:T(8,128)(2,1)} %v_ref.1), custom_call_target="tpu_custom_call" | custom-call | tf_op jit(solution)/shard_map/attention/pallas_call | solution.py:88
  113.7 5.0 %project.13 = (bf16[240,640]{1,0:T(8,128)(2,1)}, bf16[144,640]{1,0:T(8,128)(2,1)}, bf16[144,640]{1,0:T(8,128)(2,1)}, bf16[144,640]{1,0:T(8,128)(2,1)}, bf16[144,640]{1,0:T(8,128)(2,1)}) custom-call(s32[2]{0:T(128)} %pad_add_fusion.where_ref, bf16[240,2560]{1,0:T(8,128)(2,1)} %get-tuple-element.39.att_ref, bf16[240,2560]{1,0:T(8,128)(2,1)} %refs_0_.3, ...), custom_call_target="tpu_custom_call" | custom-call | tf_op jit(solution)/shard_map/project/pallas_call | solution.py:139
  118.7 3.6 %project.11 = (bf16[240,256]{1,0:T(8,128)(2,1)}, bf16[144,256]{1,0:T(8,128)(2,1)}, bf16[144,256]{1,0:T(8,128)(2,1)}, bf16[144,256]{1,0:T(8,128)(2,1)}, bf16[144,256]{1,0:T(8,128)(2,1)}) custom-call(s32[5]{0:T(128)} %stack.193.where_ref, bf16[240,2560]{1,0:T(8,128)(2,1)} %get-tuple-element.39.att_ref, bf16[240,2560]{1,0:T(8,128)(2,1)} %refs_0_.3, ...), custom_call_target="tpu_custom_call" | custom-call | tf_op jit(solution)/shard_map/project/pallas_call | solution.py:139
  122.3 3.6 %project.9 = (bf16[240,256]{1,0:T(8,128)(2,1)}, bf16[144,256]{1,0:T(8,128)(2,1)}, bf16[144,256]{1,0:T(8,128)(2,1)}, bf16[144,256]{1,0:T(8,128)(2,1)}, bf16[144,256]{1,0:T(8,128)(2,1)}) custom-call(s32[5]{0:T(128)} %stack.187.where_ref, bf16[240,2560]{1,0:T(8,128)(2,1)} %get-tuple-element.39.att_ref, bf16[240,2560]{1,0:T(8,128)(2,1)} %refs_0_.3, ...), custom_call_target="tpu_custom_call" | custom-call | tf_op jit(solution)/shard_map/project/pallas_call | solution.py:139
  126.0 4.2 %project.12 = (bf16[240,384]{1,0:T(8,128)(2,1)}, bf16[144,384]{1,0:T(8,128)(2,1)}, bf16[144,384]{1,0:T(8,128)(2,1)}, bf16[144,384]{1,0:T(8,128)(2,1)}, bf16[144,384]{1,0:T(8,128)(2,1)}) custom-call(s32[5]{0:T(128)} %stack.196.where_ref, bf16[240,2560]{1,0:T(8,128)(2,1)} %get-tuple-element.39.att_ref, bf16[240,2560]{1,0:T(8,128)(2,1)} %refs_0_.3, ...), custom_call_target="tpu_custom_call" | custom-call | tf_op jit(solution)/shard_map/project/pallas_call | solution.py:139
  130.9 3.6 %project.7 = (bf16[240,256]{1,0:T(8,128)(2,1)}, bf16[144,256]{1,0:T(8,128)(2,1)}, bf16[144,256]{1,0:T(8,128)(2,1)}, bf16[144,256]{1,0:T(8,128)(2,1)}, bf16[144,256]{1,0:T(8,128)(2,1)}) custom-call(s32[5]{0:T(128)} %stack.90.where_ref, bf16[240,2560]{1,0:T(8,128)(2,1)} %get-tuple-element.39.att_ref, bf16[240,2560]{1,0:T(8,128)(2,1)} %refs_0_.3, ...), custom_call_target="tpu_custom_call" | custom-call | tf_op jit(solution)/shard_map/project/pallas_call | solution.py:139
  136.0 4.2 %project.10 = (bf16[240,384]{1,0:T(8,128)(2,1)}, bf16[144,384]{1,0:T(8,128)(2,1)}, bf16[144,384]{1,0:T(8,128)(2,1)}, bf16[144,384]{1,0:T(8,128)(2,1)}, bf16[144,384]{1,0:T(8,128)(2,1)}) custom-call(s32[5]{0:T(128)} %stack.190.where_ref, bf16[240,2560]{1,0:T(8,128)(2,1)} %get-tuple-element.39.att_ref, bf16[240,2560]{1,0:T(8,128)(2,1)} %refs_0_.3, ...), custom_call_target="tpu_custom_call" | custom-call | tf_op jit(solution)/shard_map/project/pallas_call | solution.py:139
  140.4 4.4 %project.8 = (bf16[240,384]{1,0:T(8,128)(2,1)}, bf16[144,384]{1,0:T(8,128)(2,1)}, bf16[144,384]{1,0:T(8,128)(2,1)}, bf16[144,384]{1,0:T(8,128)(2,1)}, bf16[144,384]{1,0:T(8,128)(2,1)}) custom-call(s32[5]{0:T(128)} %stack.184.where_ref, bf16[240,2560]{1,0:T(8,128)(2,1)} %get-tuple-element.39.att_ref, bf16[240,2560]{1,0:T(8,128)(2,1)} %refs_0_.3, ...), custom_call_target="tpu_custom_call" | custom-call | tf_op jit(solution)/shard_map/project/pallas_call | solution.py:139
  144.8 3.2 %probe.3 = f32[8,2560]{1,0:T(8,128)} custom-call(s32[7]{0:T(128)} %stack.205.where_ref, s32[1,240]{1,0:T(1,128)} %bitcast.43, bf16[8,2560]{1,0:T(8,128)(2,1)} %get-tuple-element.84.probe_ref, bf16[240,640]{1,0:T(8,128)(2,1)} %get-tuple-element.69.refs_0_, bf16[240,384]{1,0:T(8,128)(2,1)} %get-tuple-element.70.refs_1_, ...), custom_call_target="tpu_custom_call" | custom-call | tf_op jit(solution)/shard_map/probe/pallas_call | solution.py:169
  154.3 7.1 %collective-permute-done.53 = f32[8,640]{1,0:T(8,128)S(1)} collective-permute-done((f32[8,640]{1,0:T(8,128)S(1)}, f32[8,640]{1,0:T(8,128)S(1)}, u32[]{:S(2)}, u32[]{:S(2)}) %collective-permute-start.53) | collective-permute-done | bytes 20512 | tf_op jit(solution)/shard_map/ppermute | solution.py:223
  163.2 3.4 %collective-permute-start.57 = (f32[8,640]{1,0:T(8,128)S(1)}, f32[8,640]{1,0:T(8,128)S(1)}, u32[]{:S(2)}, u32[]{:S(2)}) collective-permute-start(f32[8,640]{1,0:T(8,128)S(1)} %add_add_fusion.1), channel_id=1, source_target_pairs={{0,1},{1,0},{2,3},{3,2},{4,5},{5,4},{6,7},{7,6},{8,9},{9,8},{10,11... | collective-permute-start | bytes 61448 | tf_op jit(solution)/shard_map/ppermute | solution.py:223
  166.6 2.2 collective-permute-start.58
  180.3 24.1 %place.7.refs_4_ = bf16[576,2560]{1,0:T(8,128)(2,1)} custom-call(s32[5]{0:T(128)} %stack.198.where_ref, bf16[144,640]{1,0:T(8,128)(2,1)} %get-tuple-element.65.refs_0_, bf16[144,640]{1,0:T(8,128)(2,1)} %copy-done.18, bf16[144,640]{1,0:T(8,128)(2,1)} %copy-done.19, bf16[144,640]{1,0:T(8,128)(2,1)} %copy-done.20), custom_call_target="tpu_custom_call" | custom-call | tf_op jit(solution)/shard_map/place/pallas_call | solution.py:202
  204.5 15.2 %place.8.refs_4_ = bf16[576,2560]{1,0:T(8,128)(2,1)} custom-call(s32[5]{0:T(128)} %stack.195.where_ref, bf16[144,384]{1,0:T(8,128)(2,1)} %get-tuple-element.61.refs_0_, bf16[144,384]{1,0:T(8,128)(2,1)} %copy-done.22, bf16[144,384]{1,0:T(8,128)(2,1)} %copy-done.24, bf16[144,384]{1,0:T(8,128)(2,1)} %copy-done.25, ...), custom_call_target="tpu_custom_call", output_to_operand_aliasing={{}: (5, {})} | custom-call | tf_op jit(solution)/shard_map/place/pallas_call | solution.py:202
  219.7 10.9 %place.9.refs_4_ = bf16[576,2560]{1,0:T(8,128)(2,1)} custom-call(s32[5]{0:T(128)} %stack.192.where_ref, bf16[144,256]{1,0:T(8,128)(2,1)} %get-tuple-element.57.refs_0_, bf16[144,256]{1,0:T(8,128)(2,1)} %copy-done.30, bf16[144,256]{1,0:T(8,128)(2,1)} %copy-done.31, bf16[144,256]{1,0:T(8,128)(2,1)} %copy-done.32, ...), custom_call_target="tpu_custom_call", output_to_operand_aliasing={{}: (5, {})} | custom-call | tf_op jit(solution)/shard_map/place/pallas_call | solution.py:202
  231.3 15.3 %place.10.refs_4_ = bf16[576,2560]{1,0:T(8,128)(2,1)} custom-call(s32[5]{0:T(128)} %stack.189.where_ref, bf16[144,384]{1,0:T(8,128)(2,1)} %get-tuple-element.53.refs_0_, bf16[144,384]{1,0:T(8,128)(2,1)} %copy-done.21, bf16[144,384]{1,0:T(8,128)(2,1)} %copy-done.23, bf16[144,384]{1,0:T(8,128)(2,1)} %copy-done.27, ...), custom_call_target="tpu_custom_call", output_to_operand_aliasing={{}: (5, {})} | custom-call | tf_op jit(solution)/shard_map/place/pallas_call | solution.py:202
  249.3 10.9 %place.11.refs_4_ = bf16[576,2560]{1,0:T(8,128)(2,1)} custom-call(s32[5]{0:T(128)} %stack.186.where_ref, bf16[144,256]{1,0:T(8,128)(2,1)} %get-tuple-element.49.refs_0_, bf16[144,256]{1,0:T(8,128)(2,1)} %copy-done.35, bf16[144,256]{1,0:T(8,128)(2,1)} %copy-done.37, bf16[144,256]{1,0:T(8,128)(2,1)} %copy-done.38, ...), custom_call_target="tpu_custom_call", output_to_operand_aliasing={{}: (5, {})} | custom-call | tf_op jit(solution)/shard_map/place/pallas_call | solution.py:202
  261.3 3.0 collective-permute-done.61
  264.3 3.2 %collective-permute-done.62 = f32[8,640]{1,0:T(8,128)S(1)} collective-permute-done((f32[8,640]{1,0:T(8,128)S(1)}, f32[8,640]{1,0:T(8,128)S(1)}, u32[]{:S(2)}, u32[]{:S(2)}) %collective-permute-start.62) | collective-permute-done | bytes 20512 | tf_op jit(solution)/shard_map/ppermute | solution.py:223
  269.1 4.0 %collective-permute-done.16.refs_2_ = bf16[144,384]{1,0:T(8,128)(2,1)S(1)} collective-permute-done((bf16[144,384]{1,0:T(8,128)(2,1)S(1)}, bf16[144,384]{1,0:T(8,128)(2,1)S(1)}, u32[]{:S(2)}, u32[]{:S(2)}) %collective-permute-start.16) | collective-permute-done | bytes 110624 | tf_op jit(solution)/shard_map/ppermute | solution.py:223
  274.4 15.2 %place.12.refs_4_ = bf16[576,2560]{1,0:T(8,128)(2,1)} custom-call(s32[5]{0:T(128)} %stack.183.where_ref, bf16[144,384]{1,0:T(8,128)(2,1)} %get-tuple-element.45.refs_0_, bf16[144,384]{1,0:T(8,128)(2,1)} %copy-done.26, bf16[144,384]{1,0:T(8,128)(2,1)} %copy-done.28, bf16[144,384]{1,0:T(8,128)(2,1)} %copy-done.29, ...), custom_call_target="tpu_custom_call", output_to_operand_aliasing={{}: (5, {})} | custom-call | tf_op jit(solution)/shard_map/place/pallas_call | solution.py:202
  290.3 10.7 %place.13 = bf16[576,2560]{1,0:T(8,128)(2,1)} custom-call(s32[5]{0:T(128)} %stack.85.where_ref, bf16[144,256]{1,0:T(8,128)(2,1)} %get-tuple-element.41.refs_0_, bf16[144,256]{1,0:T(8,128)(2,1)} %copy-done.33, bf16[144,256]{1,0:T(8,128)(2,1)} %copy-done.34, bf16[144,256]{1,0:T(8,128)(2,1)} %copy-done.36, ...), custom_call_target="tpu_custom_call", output_to_operand_aliasing={{}: (5, {})} | custom-call | tf_op jit(solution)/shard_map/place/pallas_call | solution.py:202
  (264 shorter events, 65.1 us)
Async XLA Ops:
  1.7 21.6 %collective-permute-start.9 = (bf16[640,384]{1,0:T(8,128)(2,1)S(1)}, bf16[640,384]{1,0:T(8,128)(2,1)S(1)}, u32[]{:S(2)}, u32[]{:S(2)}) collective-permute-start(bf16[640,384]{1,0:T(8,128)(2,1)S(1)} %constant_dynamic-slice_fusion.6), channel_id=1, source_target_pairs={{0,1},{1,2},{2,3},{3,0},{4,5},{5,6},{6,7},{7,4},{8,9},{9,10},{10,1... | collective-permute-start | bytes 1474568 | tf_op jit(solution)/shard_map/ppermute | solution.py:313
  4.4 17.4 %collective-permute-start = (bf16[640,256]{1,0:T(8,128)(2,1)S(1)}, bf16[640,256]{1,0:T(8,128)(2,1)S(1)}, u32[]{:S(2)}, u32[]{:S(2)}) collective-permute-start(bf16[640,256]{1,0:T(8,128)(2,1)S(1)} %constant_dynamic-slice_fusion.7), channel_id=1, source_target_pairs={{0,1},{1,2},{2,3},{3,0},{4,5},{5,6},{6,7},{7,4},{8,9},{9,10},{10,1... | collective-permute-start | bytes 983048 | tf_op jit(solution)/shard_map/ppermute | solution.py:313
  21.8 25.1 %collective-permute-start.1 = (bf16[640,256]{1,0:T(8,128)(2,1)S(1)}, bf16[640,256]{1,0:T(8,128)(2,1)}, u32[]{:S(2)}, u32[]{:S(2)}) collective-permute-start(bf16[640,256]{1,0:T(8,128)(2,1)S(1)} %collective-permute-done.refs_0_), channel_id=1, source_target_pairs={{0,1},{1,2},{2,3},{3,0},{4,5},{5,6},{6,7},{7,4},{8,9},{9,10},{10,1... | collective-permute-start | bytes 983048 | tf_op jit(solution)/shard_map/ppermute | solution.py:313
  23.4 25.3 %collective-permute-start.10 = (bf16[640,384]{1,0:T(8,128)(2,1)S(1)}, bf16[640,384]{1,0:T(8,128)(2,1)S(1)}, u32[]{:S(2)}, u32[]{:S(2)}) collective-permute-start(bf16[640,384]{1,0:T(8,128)(2,1)S(1)} %collective-permute-done.9.refs_0_), channel_id=1, source_target_pairs={{0,1},{1,2},{2,3},{3,0},{4,5},{5,6},{6,7},{7,4},{8,9},{9,10},{10,1... | collective-permute-start | bytes 1474568 | tf_op jit(solution)/shard_map/ppermute | solution.py:313
  27.6 19.8 %collective-permute-start.30 = (bf16[640,256]{1,0:T(8,128)(2,1)S(1)}, bf16[640,256]{1,0:T(8,128)(2,1)S(1)}, u32[]{:S(2)}, u32[]{:S(2)}) collective-permute-start(bf16[640,256]{1,0:T(8,128)(2,1)S(1)} %collective-permute-done.refs_0_), channel_id=1, source_target_pairs={{0,16},{16,0},{1,17},{17,1},{2,18},{18,2},{3,19},{19,3},{4,20},{20... | collective-permute-start | bytes 983048 | tf_op jit(solution)/shard_map/ppermute | solution.py:316
  31.7 13.5 %collective-permute-start.49 = (f32[8,640]{1,0:T(8,128)S(1)}, f32[8,640]{1,0:T(8,128)S(1)}, u32[]{:S(2)}, u32[]{:S(2)}) collective-permute-start(f32[8,640]{1,0:T(8,128)S(1)} %add_add_fusion.3), channel_id=1, source_target_pairs={{0,2},{1,3},{2,0},{3,1},{4,6},{5,7},{6,4},{7,5},{8,10},{9,11},{10,... | collective-permute-start | bytes 61448 | tf_op jit(solution)/shard_map/ppermute | solution.py:223
  45.2 14.1 %collective-permute-start.36 = (bf16[640,384]{1,0:T(8,128)(2,1)S(1)}, bf16[640,384]{1,0:T(8,128)(2,1)S(1)}, u32[]{:S(2)}, u32[]{:S(2)}) collective-permute-start(bf16[640,384]{1,0:T(8,128)(2,1)S(1)} %collective-permute-done.9.refs_0_), channel_id=1, source_target_pairs={{0,16},{16,0},{1,17},{17,1},{2,18},{18,2},{3,19},{19,3},{4,20},{20... | collective-permute-start | bytes 1474568 | tf_op jit(solution)/shard_map/ppermute | solution.py:316
  47.4 15.6 %collective-permute-start.18 = (bf16[640,256]{1,0:T(8,128)(2,1)}, bf16[640,256]{1,0:T(8,128)(2,1)S(1)}, u32[]{:S(2)}, u32[]{:S(2)}) collective-permute-start(bf16[640,256]{1,0:T(8,128)(2,1)} %collective-permute-done.1.refs_0_), channel_id=1, source_target_pairs={{0,16},{16,0},{1,17},{17,1},{2,18},{18,2},{3,19},{19,3},{4,20},{20... | collective-permute-start | bytes 983048 | tf_op jit(solution)/shard_map/ppermute | solution.py:316
  48.7 16.9 %collective-permute-start.11 = (bf16[640,384]{1,0:T(8,128)(2,1)S(1)}, bf16[640,384]{1,0:T(8,128)(2,1)S(1)}, u32[]{:S(2)}, u32[]{:S(2)}) collective-permute-start(bf16[640,384]{1,0:T(8,128)(2,1)S(1)} %collective-permute-done.10.refs_0_), channel_id=1, source_target_pairs={{0,1},{1,2},{2,3},{3,0},{4,5},{5,6},{6,7},{7,4},{8,9},{9,10},{10,1... | collective-permute-start | bytes 1474568 | tf_op jit(solution)/shard_map/ppermute | solution.py:313
  63.1 31.2 %collective-permute-start.24 = (bf16[640,384]{1,0:T(8,128)(2,1)S(1)}, bf16[640,384]{1,0:T(8,128)(2,1)S(1)}, u32[]{:S(2)}, u32[]{:S(2)}) collective-permute-start(bf16[640,384]{1,0:T(8,128)(2,1)S(1)} %collective-permute-done.10.refs_0_), channel_id=1, source_target_pairs={{0,16},{16,0},{1,17},{17,1},{2,18},{18,2},{3,19},{19,3},{4,20},{20... | collective-permute-start | bytes 1474568 | tf_op jit(solution)/shard_map/ppermute | solution.py:316
  65.6 29.3 %collective-permute-start.12 = (bf16[640,384]{1,0:T(8,128)(2,1)S(1)}, bf16[640,384]{1,0:T(8,128)(2,1)S(1)}, u32[]{:S(2)}, u32[]{:S(2)}) collective-permute-start(bf16[640,384]{1,0:T(8,128)(2,1)S(1)} %collective-permute-done.11.refs_0_), channel_id=1, source_target_pairs={{0,16},{16,0},{1,17},{17,1},{2,18},{18,2},{3,19},{19,3},{4,20},{20... | collective-permute-start | bytes 1474568 | tf_op jit(solution)/shard_map/ppermute | solution.py:316
  66.4 46.3 %collective-permute-start.38 = (bf16[640,384]{1,0:T(8,128)(2,1)S(1)}, bf16[640,384]{1,0:T(8,128)(2,1)}, u32[]{:S(2)}, u32[]{:S(2)}) collective-permute-start(bf16[640,384]{1,0:T(8,128)(2,1)S(1)} %collective-permute-done.36.refs_1_), channel_id=1, source_target_pairs={{0,4},{4,0},{8,12},{12,8},{1,5},{5,1},{9,13},{13,9},{2,6},{6,2},{1... | collective-permute-start | bytes 1474568 | tf_op jit(solution)/shard_map/ppermute | solution.py:223
  71.8 22.5 %collective-permute-start.3 = (bf16[640,256]{1,0:T(8,128)(2,1)S(1)}, bf16[640,256]{1,0:T(8,128)(2,1)S(1)}, u32[]{:S(2)}, u32[]{:S(2)}) collective-permute-start(bf16[640,256]{1,0:T(8,128)(2,1)S(1)} %collective-permute-done.2.refs_0_), channel_id=1, source_target_pairs={{0,16},{16,0},{1,17},{17,1},{2,18},{18,2},{3,19},{19,3},{4,20},{20... | collective-permute-start | bytes 983048 | tf_op jit(solution)/shard_map/ppermute | solution.py:316
  72.5 22.3 %collective-permute-start.4 = (bf16[640,256]{1,0:T(8,128)(2,1)S(1)}, bf16[640,256]{1,0:T(8,128)(2,1)S(1)}, u32[]{:S(2)}, u32[]{:S(2)}) collective-permute-start(bf16[640,256]{1,0:T(8,128)(2,1)S(1)} %collective-permute-done.2.refs_0_), channel_id=1, source_target_pairs={{0,4},{4,0},{8,12},{12,8},{1,5},{5,1},{9,13},{13,9},{2,6},{6,2},{1... | collective-permute-start | bytes 983048 | tf_op jit(solution)/shard_map/ppermute | solution.py:223
  94.3 40.3 %collective-permute-start.25 = (bf16[640,384]{1,0:T(8,128)(2,1)S(1)}, bf16[640,384]{1,0:T(8,128)(2,1)}, u32[]{:S(2)}, u32[]{:S(2)}) collective-permute-start(bf16[640,384]{1,0:T(8,128)(2,1)S(1)} %collective-permute-done.10.refs_0_), channel_id=1, source_target_pairs={{0,4},{4,0},{8,12},{12,8},{1,5},{5,1},{9,13},{13,9},{2,6},{6,2},{1... | collective-permute-start | bytes 1474568 | tf_op jit(solution)/shard_map/ppermute | solution.py:223
  94.3 40.5 %collective-permute-start.26 = (bf16[640,384]{1,0:T(8,128)(2,1)S(1)}, bf16[640,384]{1,0:T(8,128)(2,1)}, u32[]{:S(2)}, u32[]{:S(2)}) collective-permute-start(bf16[640,384]{1,0:T(8,128)(2,1)S(1)} %collective-permute-done.24.refs_1_), channel_id=1, source_target_pairs={{0,4},{4,0},{8,12},{12,8},{1,5},{5,1},{9,13},{13,9},{2,6},{6,2},{1... | collective-permute-start | bytes 1474568 | tf_op jit(solution)/shard_map/ppermute | solution.py:223
  94.8 45.6 %collective-permute-start.13 = (bf16[640,384]{1,0:T(8,128)(2,1)S(1)}, bf16[640,384]{1,0:T(8,128)(2,1)}, u32[]{:S(2)}, u32[]{:S(2)}) collective-permute-start(bf16[640,384]{1,0:T(8,128)(2,1)S(1)} %collective-permute-done.11.refs_0_), channel_id=1, source_target_pairs={{0,4},{4,0},{8,12},{12,8},{1,5},{5,1},{9,13},{13,9},{2,6},{6,2},{1... | collective-permute-start | bytes 1474568 | tf_op jit(solution)/shard_map/ppermute | solution.py:223
  95.5 44.9 %collective-permute-start.14 = (bf16[640,384]{1,0:T(8,128)(2,1)S(1)}, bf16[640,384]{1,0:T(8,128)(2,1)}, u32[]{:S(2)}, u32[]{:S(2)}) collective-permute-start(bf16[640,384]{1,0:T(8,128)(2,1)S(1)} %collective-permute-done.12.refs_1_), channel_id=1, source_target_pairs={{0,4},{4,0},{8,12},{12,8},{1,5},{5,1},{9,13},{13,9},{2,6},{6,2},{1... | collective-permute-start | bytes 1474568 | tf_op jit(solution)/shard_map/ppermute | solution.py:223
  112.7 17.5 %collective-permute-start.5 = (bf16[640,256]{1,0:T(8,128)(2,1)}, bf16[640,256]{1,0:T(8,128)(2,1)S(1)}, u32[]{:S(2)}, u32[]{:S(2)}) collective-permute-start(bf16[640,256]{1,0:T(8,128)(2,1)} %copy-done.15), channel_id=1, source_target_pairs={{0,4},{4,0},{8,12},{12,8},{1,5},{5,1},{9,13},{13,9},{2,6},{6,2},{1... | collective-permute-start | bytes 983048 | tf_op jit(solution)/shard_map/ppermute | solution.py:223
  130.2 31.9 %collective-permute-start.42 = (bf16[144,640]{1,0:T(8,128)(2,1)S(1)}, bf16[144,640]{1,0:T(8,128)(2,1)S(1)}, u32[]{:S(2)}, u32[]{:S(2)}) collective-permute-start(bf16[144,640]{1,0:T(8,128)(2,1)S(1)} %copy-done.41), channel_id=1, source_target_pairs={{0,4},{4,0},{8,12},{12,8},{1,5},{5,1},{9,13},{13,9},{2,6},{6,2},{1... | collective-permute-start | bytes 552968 | tf_op jit(solution)/shard_map/ppermute | solution.py:223
  134.6 15.1 %collective-permute-start.51 = (f32[8,640]{1,0:T(8,128)S(1)}, f32[8,640]{1,0:T(8,128)S(1)}, u32[]{:S(2)}, u32[]{:S(2)}) collective-permute-start(f32[8,640]{1,0:T(8,128)S(1)} %get-tuple-element.77), channel_id=1, source_target_pairs={{0,4},{4,0},{8,12},{12,8},{1,5},{5,1},{9,13},{13,9},{2,6},{6,2},{1... | collective-permute-start | bytes 61448 | tf_op jit(solution)/shard_map/ppermute | solution.py:223
  134.8 15.8 %collective-permute-start.52 = (f32[8,640]{1,0:T(8,128)S(1)}, f32[8,640]{1,0:T(8,128)S(1)}, u32[]{:S(2)}, u32[]{:S(2)}) collective-permute-start(f32[8,640]{1,0:T(8,128)S(1)} %get-tuple-element.77), channel_id=1, source_target_pairs={{0,8},{4,12},{8,0},{12,4},{1,9},{5,13},{9,1},{13,5},{2,10},{6,14},... | collective-permute-start | bytes 61448 | tf_op jit(solution)/shard_map/ppermute | solution.py:223
  151.5 15.1 %collective-permute-start.44 = (bf16[144,640]{1,0:T(8,128)(2,1)S(1)}, bf16[144,640]{1,0:T(8,128)(2,1)S(1)}, u32[]{:S(2)}, u32[]{:S(2)}) collective-permute-start(bf16[144,640]{1,0:T(8,128)(2,1)S(1)} %copy-done.39), channel_id=1, source_target_pairs={{0,12},{4,8},{8,4},{12,0},{1,13},{5,9},{9,5},{13,1},{2,14},{6,10},... | collective-permute-start | bytes 552968 | tf_op jit(solution)/shard_map/ppermute | solution.py:223
  153.3 15.5 %collective-permute-start.33 = (bf16[144,256]{1,0:T(8,128)(2,1)S(1)}, bf16[144,256]{1,0:T(8,128)(2,1)S(1)}, u32[]{:S(2)}, u32[]{:S(2)}) collective-permute-start(bf16[144,256]{1,0:T(8,128)(2,1)S(1)} %copy-done.59), channel_id=1, source_target_pairs={{0,4},{4,0},{8,12},{12,8},{1,5},{5,1},{9,13},{13,9},{2,6},{6,2},{1... | collective-permute-start | bytes 221192 | tf_op jit(solution)/shard_map/ppermute | solution.py:223
  173.4 73.2 %collective-permute-start.21 = (bf16[144,256]{1,0:T(8,128)(2,1)S(1)}, bf16[144,256]{1,0:T(8,128)(2,1)S(1)}, u32[]{:S(2)}, u32[]{:S(2)}) collective-permute-start(bf16[144,256]{1,0:T(8,128)(2,1)S(1)} %copy-done.56), channel_id=1, source_target_pairs={{0,4},{4,0},{8,12},{12,8},{1,5},{5,1},{9,13},{13,9},{2,6},{6,2},{1... | collective-permute-start | bytes 221192 | tf_op jit(solution)/shard_map/ppermute | solution.py:223
  175.5 72.0 %collective-permute-start.22 = (bf16[144,256]{1,0:T(8,128)(2,1)S(1)}, bf16[144,256]{1,0:T(8,128)(2,1)S(1)}, u32[]{:S(2)}, u32[]{:S(2)}) collective-permute-start(bf16[144,256]{1,0:T(8,128)(2,1)S(1)} %copy-done.55), channel_id=1, source_target_pairs={{0,8},{4,12},{8,0},{12,4},{1,9},{5,13},{9,1},{13,5},{2,10},{6,14},... | collective-permute-start | bytes 221192 | tf_op jit(solution)/shard_map/ppermute | solution.py:223
  176.9 71.8 %collective-permute-start.23 = (bf16[144,256]{1,0:T(8,128)(2,1)S(1)}, bf16[144,256]{1,0:T(8,128)(2,1)S(1)}, u32[]{:S(2)}, u32[]{:S(2)}) collective-permute-start(bf16[144,256]{1,0:T(8,128)(2,1)S(1)} %copy-done.54), channel_id=1, source_target_pairs={{0,12},{4,8},{8,4},{12,0},{1,13},{5,9},{9,5},{13,1},{2,14},{6,10},... | collective-permute-start | bytes 221192 | tf_op jit(solution)/shard_map/ppermute | solution.py:223
  178.1 52.5 %collective-permute-start.29 = (bf16[144,384]{1,0:T(8,128)(2,1)S(1)}, bf16[144,384]{1,0:T(8,128)(2,1)S(1)}, u32[]{:S(2)}, u32[]{:S(2)}) collective-permute-start(bf16[144,384]{1,0:T(8,128)(2,1)S(1)} %copy-done.45), channel_id=1, source_target_pairs={{0,12},{4,8},{8,4},{12,0},{1,13},{5,9},{9,5},{13,1},{2,14},{6,10},... | collective-permute-start | bytes 331784 | tf_op jit(solution)/shard_map/ppermute | solution.py:223
  180.2 80.3 %collective-permute-start.60 = (f32[8,640]{1,0:T(8,128)S(1)}, f32[8,640]{1,0:T(8,128)S(1)}, u32[]{:S(2)}, u32[]{:S(2)}) collective-permute-start(f32[8,640]{1,0:T(8,128)S(1)} %get-tuple-element.79), channel_id=1, source_target_pairs={{0,4},{4,0},{8,12},{12,8},{1,5},{5,1},{9,13},{13,9},{2,6},{6,2},{1... | collective-permute-start | bytes 61448 | tf_op jit(solution)/shard_map/ppermute | solution.py:223
  230.7 59.0 %collective-permute-start.6 = (bf16[144,256]{1,0:T(8,128)(2,1)S(1)}, bf16[144,256]{1,0:T(8,128)(2,1)S(1)}, u32[]{:S(2)}, u32[]{:S(2)}) collective-permute-start(bf16[144,256]{1,0:T(8,128)(2,1)S(1)} %copy-done.53), channel_id=1, source_target_pairs={{0,4},{4,0},{8,12},{12,8},{1,5},{5,1},{9,13},{13,9},{2,6},{6,2},{1... | collective-permute-start | bytes 221192 | tf_op jit(solution)/shard_map/ppermute | solution.py:223
  246.7 43.0 %collective-permute-start.7 = (bf16[144,256]{1,0:T(8,128)(2,1)S(1)}, bf16[144,256]{1,0:T(8,128)(2,1)S(1)}, u32[]{:S(2)}, u32[]{:S(2)}) collective-permute-start(bf16[144,256]{1,0:T(8,128)(2,1)S(1)} %copy-done.52), channel_id=1, source_target_pairs={{0,8},{4,12},{8,0},{12,4},{1,9},{5,13},{9,1},{13,5},{2,10},{6,14},... | collective-permute-start | bytes 221192 | tf_op jit(solution)/shard_map/ppermute | solution.py:223
  247.5 42.2 %collective-permute-start.8 = (bf16[144,256]{1,0:T(8,128)(2,1)S(1)}, bf16[144,256]{1,0:T(8,128)(2,1)S(1)}, u32[]{:S(2)}, u32[]{:S(2)}) collective-permute-start(bf16[144,256]{1,0:T(8,128)(2,1)S(1)} %copy-done.51), channel_id=1, source_target_pairs={{0,12},{4,8},{8,4},{12,0},{1,13},{5,9},{9,5},{13,1},{2,14},{6,10},... | collective-permute-start | bytes 221192 | tf_op jit(solution)/shard_map/ppermute | solution.py:223
  (91 other events, 1631.3 us)

commit v2 on v0

v2 whole, which is shorter than its diff:
```python
import functools

import jax
import jax.numpy as jnp
from jax import lax
from jax.experimental import pallas as pl
from jax.experimental.pallas import tpu as pltpu
from jax.sharding import PartitionSpec as P

HS = 128
CLASSES = 8
LMAX = 48
LANES = 128
PARTS_OF_COLUMNS = (3, 2)

VMEM = pl.BlockSpec(memory_space=pltpu.VMEM)
ANY = pl.BlockSpec(memory_space=pl.ANY)
SMALL = pltpu.CompilerParams(vmem_limit_bytes=12 * 2**20)
F32, BF16, I32 = jnp.float32, jnp.bfloat16, jnp.int32
NT = (((1,), (1,)), ((), ()))


def near(x):
    return pltpu.with_memory_space_constraint(x, pltpu.VMEM)


def is_pow2(n):
    return n & (n - 1) == 0


def lanes_at(start, width):
    return pl.ds(pl.multiple_of(start, LANES), width)


def peer(me, j, n):
    return me ^ j if is_pow2(n) else lax.rem(me + j, n)


def source(me, j, n):
    return me ^ j if is_pow2(n) else lax.rem(me + n - j, n)


def mismatch_of(logits, label_row, tok_count):
    exponent = jnp.exp(logits)
    likelihood = exponent / jnp.sum(exponent, axis=0, keepdims=True)
    one_hot = (lax.broadcasted_iota(I32, logits.shape, 0) == label_row).astype(F32)
    return ((likelihood - one_hot) / tok_count).astype(BF16)


def attention_kernel(
    prot_count, slot_count, group, len_ref, dest_ref, q_ref, k_ref, v_ref, att_ref, sel_ref, mask_ref
):
    rows = q_ref.shape[0]

    @pl.when(pl.program_id(0) == 0)
    def _():
        starts = []
        total = 0
        for p in range(prot_count):
            starts.append(total)
            total = total + len_ref[p]
        row = lax.broadcasted_iota(I32, (rows, rows), 0)
        col = lax.broadcasted_iota(I32, (rows, rows), 1)
        row_low, row_high = jnp.zeros_like(row), jnp.zeros_like(row)
        for p in range(prot_count):
            inside = (row >= starts[p]) & (row < starts[p] + len_ref[p])
            row_low = jnp.where(inside, starts[p], row_low)
            row_high = jnp.where(inside, starts[p] + len_ref[p], row_high)
        mask_ref[...] = ((col >= row_low) & (col < row_high)).astype(F32)

        ranks = []
        for p in range(prot_count):
            rank = 0
            for q in range(p):
                rank = rank + (dest_ref[q] == dest_ref[p]).astype(I32)
            ranks.append(rank)
        t_row = lax.broadcasted_iota(I32, (LMAX, rows), 0)
        t_col = lax.broadcasted_iota(I32, (LMAX, rows), 1)
        me = lax.axis_index("dp")
        for j in range(group):
            target = peer(me, j, group)
            for r in range(slot_count):
                start, length = jnp.int32(0), jnp.int32(0)
                for p in range(prot_count):
                    hit = (dest_ref[p] == target) & (ranks[p] == r)
                    start = jnp.where(hit, starts[p], start)
                    length = jnp.where(hit, len_ref[p], length)
                chosen = (t_col == t_row + start) & (t_row < length)
                block = (j * slot_count + r) * LMAX
                sel_ref[block : block + LMAX, :] = chosen.astype(F32).astype(BF16)

    width = q_ref.shape[1]
    for h in range(width // HS):
        cols = slice(h * HS, (h + 1) * HS)
        scores = lax.dot_general(
            q_ref[:, cols], k_ref[:, cols], NT, preferred_element_type=F32
        ) * HS ** (-0.5)
        weights = jnp.where(mask_ref[...] > 0, jnp.exp(scores), 0.0)
        total = jnp.sum(weights, axis=1, keepdims=True)
        low = (weights / total).astype(BF16)
        spot = lanes_at(pl.program_id(0) * width + h * HS, HS)
        att_ref[:, spot] = jnp.dot(low, v_ref[:, cols], preferred_element_type=F32).astype(BF16)


def attention(projected, lengths, destination, group, slot_count):
    rows, width = projected.shape
    hidden = width // 3
    per = 4 * HS if hidden % (4 * HS) == 0 else HS
    steps = hidden // per
    sel_rows = group * slot_count * LMAX
    return pl.pallas_call(
        functools.partial(attention_kernel, lengths.shape[0], slot_count, group),
        grid_spec=pltpu.PrefetchScalarGridSpec(
            num_scalar_prefetch=2,
            grid=(steps,),
            in_specs=[
                pl.BlockSpec((rows, per), lambda i, *_: (0, i)),
                pl.BlockSpec((rows, per), lambda i, *_: (0, i + steps)),
                pl.BlockSpec((rows, per), lambda i, *_: (0, i + 2 * steps)),
            ],
            out_specs=[VMEM, VMEM],
            scratch_shapes=[pltpu.VMEM((rows, rows), F32)],
        ),
        out_shape=[pltpu.VMEM((rows, hidden), BF16), pltpu.VMEM((sel_rows, rows), BF16)],
        name="attention",
        compiler_params=SMALL,
    )(lengths, destination, projected, projected, projected)


def swap(x, axis, j):
    n = lax.axis_size(axis)
    pairs = [(i, int(i ^ j) if is_pow2(n) else (i + j) % n) for i in range(n)]
    return near(lax.ppermute(x, axis, pairs))


def rotate(x, axis):
    n = lax.axis_size(axis)
    return near(lax.ppermute(x, axis, [(i, (i + 1) % n) for i in range(n)]))


def add_kernel(*refs):
    terms, out = [r[...] for r in refs[:-1]], refs[-1]
    while len(terms) > 1:
        terms = [a + b for a, b in zip(terms[::2], terms[1::2])]
    out[...] = terms[0]


def add_up(terms):
    return near(
        pl.pallas_call(
            add_kernel,
            in_specs=[VMEM] * len(terms),
            out_specs=VMEM,
            out_shape=pltpu.VMEM(terms[0].shape, terms[0].dtype),
            name="add_up",
            compiler_params=SMALL,
        )(*terms)
    )


def my_share(cores):
    return lax.axis_index("parts") * cores + lax.rem(lax.axis_index("dp"), cores)


def shard_of(step, ring):
    return lax.rem(lax.axis_index("shard") + ring - step, ring)


def prepare_kernel(splits, cores, w_ref, *refs):
    *outs, held, sem = refs
    depth = held.shape[0]
    copy = pltpu.make_async_copy(
        w_ref.at[pl.ds(pl.multiple_of(my_share(cores) * depth, 16), depth), :], held, sem
    )
    copy.start()
    copy.wait()
    off = 0
    for out, width in zip(outs, splits):
        out[...] = held[:, off : off + width]
        off += width


def prepare(out_weight, splits, cores, depth):
    columns = out_weight.shape[1]
    return pl.pallas_call(
        functools.partial(prepare_kernel, splits, cores),
        in_specs=[ANY],
        out_specs=[VMEM] * len(splits),
        out_shape=[pltpu.VMEM((depth, w), BF16) for w in splits],
        scratch_shapes=[pltpu.VMEM((depth, columns), BF16), pltpu.SemaphoreType.DMA],
        name="prepare",
        compiler_params=SMALL,
    )(pltpu.with_memory_space_constraint(out_weight, pltpu.HBM))


def share_rows(count, cores, depth):
    mine = my_share(cores)
    return [r * depth for r in (mine, mine ^ cores, mine ^ 1, mine ^ cores ^ 1)][:count]


def first_probe_kernel(ring, columns, blocks, resid_ref, probe_ref, label_ref, *refs):
    hidden, (grad_ref, logits_ref) = refs[:-2], refs[-2:]
    tok_count = resid_ref.shape[0]
    logits = lax.dot_general(probe_ref[0], resid_ref[...], NT, preferred_element_type=F32)
    mismatch = mismatch_of(logits, label_ref[...], tok_count)
    grad_ref[...] = jnp.dot(mismatch, resid_ref[...], preferred_element_type=F32)
    logits_ref[...] = partial_logits(ring, columns, blocks, probe_ref, hidden)


def partial_logits(ring, columns, blocks, probe_ref, hidden):
    total = None
    for (step, off, width), rows in zip(blocks, hidden):
        probe = probe_ref[1, :, lanes_at(shard_of(step, ring) * columns + off, width)]
        part = lax.dot_general(probe, rows[...], NT, preferred_element_type=F32)
        total = part if total is None else total + part
    return total


def first_probe(blocks, residual, probes, label_row, hidden, ring, columns):
    rows, width = residual.shape
    return pl.pallas_call(
        functools.partial(first_probe_kernel, ring, columns, blocks),
        in_specs=[VMEM] * (3 + len(hidden)),
        out_specs=[VMEM] * 2,
        out_shape=[pltpu.VMEM((CLASSES, width), F32), pltpu.VMEM((CLASSES, rows), F32)],
        name="first_probe",
        compiler_params=SMALL,
    )(residual, probes, label_row, *hidden)


def second_probe_kernel(group, ring, columns, blocks, known, probe_ref, label_ref, grad_ref, logits_ref, *refs):
    hidden, outs, grads = refs[: len(blocks)], refs[len(blocks) : -1], refs[-1]
    tok_count = label_ref.shape[1]
    rest = partial_logits(ring, columns, blocks[known:], probe_ref, hidden[known:])
    mismatch = mismatch_of(logits_ref[...] + rest, label_ref[...], tok_count)
    grads[0:CLASSES, :] = grad_ref[...]
    for (step, off, width), rows in zip(blocks, hidden):
        spot = lanes_at(shard_of(step, ring) * columns + off, width)
        grads[CLASSES:, spot] = jnp.dot(mismatch, rows[...], preferred_element_type=F32)
    me = lax.axis_index("dp")
    for j, out in enumerate(outs):
        width = out.shape[1]
        out[...] = grads[:, lanes_at(peer(me, j, group) * width, width)]


def second_probe(blocks, known, probes, label_row, first, logits, hidden, group, ring, columns):
    width = first.shape[1]
    return pl.pallas_call(
        functools.partial(second_probe_kernel, group, ring, columns, blocks, known),
        in_specs=[VMEM] * (4 + len(hidden)),
        out_specs=[VMEM] * group,
        out_shape=[pltpu.VMEM((2 * CLASSES, width // group), F32)] * group,
        scratch_shapes=[pltpu.VMEM((2 * CLASSES, width), F32)],
        name="second_probe",
        compiler_params=SMALL,
    )(probes, label_row, first, logits, *hidden)


def gradient_kernel(group, *refs):
    pieces, out_ref = refs[:-1], refs[-1]
    me = lax.axis_index("dp")
    width = pieces[0].shape[1]
    for j, piece in enumerate(pieces):
        spot = lanes_at(peer(me, j, group) * width, width)
        out_ref[0, :, spot] = piece[0:CLASSES, :]
        out_ref[1, :, spot] = piece[CLASSES:, :]


def gradient(pieces):
    group = len(pieces)
    return pl.pallas_call(
        functools.partial(gradient_kernel, group),
        in_specs=[VMEM] * group,
        out_specs=VMEM,
        out_shape=jax.ShapeDtypeStruct((2, CLASSES, group * pieces[0].shape[1]), F32),
        name="gradient",
        compiler_params=SMALL,
    )(*pieces)


def project_kernel(blocks, group, ring, cores, columns, att_ref, resid_ref, sel_ref, *refs):
    pieces, sends, hid_ref = refs[: -group - 1], refs[-group - 1 : -1], refs[-1]
    span = sel_ref.shape[0] // group
    done, at = 0, 0
    for step, off, width, count in blocks:
        depth = pieces[done].shape[0]
        total = None
        for row, piece in zip(share_rows(count, cores, depth), pieces[done : done + count]):
            rows = att_ref[...] if count == 1 else att_ref[:, lanes_at(row, depth)]
            part = jnp.dot(rows, piece[...], preferred_element_type=F32)
            total = part if total is None else total + part
        resid = resid_ref[:, lanes_at(shard_of(step, ring) * columns + off, width)]
        hidden = (total + resid.astype(F32)).astype(BF16)
        hid_ref[:, at : at + width] = hidden
        for j, send in enumerate(sends):
            send[:, at : at + width] = jnp.dot(
                sel_ref[j * span : (j + 1) * span, :], hidden, preferred_element_type=F32
            ).astype(BF16)
        done += count
        at += width


def project(blocks, att, residual, sel, pieces, group, ring, cores, columns):
    span = sel.shape[0] // group
    width = sum(w for _, _, w, _ in blocks)
    return pl.pallas_call(
        functools.partial(project_kernel, blocks, group, ring, cores, columns),
        in_specs=[VMEM] * (3 + len(pieces)),
        out_specs=[VMEM] * (group + 1),
        out_shape=[pltpu.VMEM((span, width), BF16)] * group + [pltpu.VMEM((att.shape[0], width), BF16)],
        name="project",
        compiler_params=SMALL,
    )(att, residual, sel, *pieces)


def place_kernel(sets, group, ring, columns, *refs):
    blocks, out_ref, sems = refs[: group * len(sets)], refs[-2], refs[-1]
    me = lax.axis_index("dp")
    stores = []
    for s, (step, off, width) in enumerate(sets):
        for j in range(group):
            block = blocks[s * group + j]
            span = block.shape[0]
            stores.append(
                pltpu.make_async_copy(
                    block,
                    out_ref.at[
                        pl.ds(pl.multiple_of(source(me, j, group) * span, 16), span),
                        lanes_at(shard_of(step, ring) * columns + off, width),
                    ],
                    sems.at[len(stores)],
                )
            )
    for store in stores:
        store.start()
    for store in stores:
        store.wait()


def place(sets, blocks, out, shape, group, ring, columns):
    held = [] if out is None else [out]
    return pl.pallas_call(
        functools.partial(place_kernel, sets, group, ring, columns),
        in_specs=[VMEM] * len(blocks) + [ANY] * len(held),
        out_specs=ANY,
        out_shape=jax.ShapeDtypeStruct(shape, BF16),
        scratch_shapes=[pltpu.SemaphoreType.DMA((len(blocks),))],
        input_output_aliases={len(blocks): 0} if held else {},
        name="place",
        compiler_params=SMALL,
    )(*blocks, *held)


def splits_of(columns):
    whole = sum(PARTS_OF_COLUMNS) * LANES
    if columns % whole:
        return (columns,)
    return tuple(columns // sum(PARTS_OF_COLUMNS) * p for p in PARTS_OF_COLUMNS)


def is_fast(mesh_shape, columns, inner):
    parts, group, ring = mesh_shape["parts"], mesh_shape["dp"], mesh_shape["shard"]
    if (parts, group, ring) != (2, 4, 4):
        return False
    return len(splits_of(columns)) == 2 and inner % (parts * 2 * LANES) == 0


def per_device_fast(projected, residual, out_weight, probe_weight, labels, lengths, destination):
    group, ring = lax.axis_size("dp"), lax.axis_size("shard")
    cores = 2
    slot_count = -(-lengths.shape[1] // group)
    inner, columns = out_weight.shape
    splits = splits_of(columns)
    offs = (0, splits[0])
    depth = inner // (2 * cores)
    shape = (group * slot_count * LMAX, residual.shape[1])
    probes = jnp.swapaxes(probe_weight, 1, 2)
    label_row = labels.reshape(1, -1)

    def fill(piece):
        other = swap(piece, "parts", 1)
        return [piece, other, swap(piece, "dp", 1), swap(other, "dp", 1)]

    def send(made):
        *sends, hid = [near(m) for m in made]
        hidden.append(hid)
        return [sends[0]] + [swap(sends[j], "dp", j) for j in range(1, group)]

    def chunk(step, i, count=4):
        return (step, offs[i], splits[i], count)

    tail = (group, ring, cores, columns)
    hidden = []
    held = [near(h) for h in prepare(out_weight, splits, cores, depth)]
    att, sel = map(near, attention(projected, lengths[0], destination[0], group, slot_count))
    residual, weight_here = near(residual), near(out_weight)

    ring_a, ring_b = [held[0]], [held[1]]
    for _ in range(1, ring):
        ring_a.append(rotate(ring_a[-1], "shard"))
        ring_b.append(rotate(ring_b[-1], "shard"))
    chunks = [[fill(ring_a[s]), fill(ring_b[s])] if s else None for s in range(ring)]
    made = project(((0, 0, columns, 1),), att, residual, sel, [weight_here], *tail)
    got0 = send(made)
    made = project((chunk(1, 0), chunk(1, 1)), att, residual, sel, chunks[1][0] + chunks[1][1], *tail)
    got1 = send(made)
    made = project((chunk(2, 0), chunk(2, 1)), att, residual, sel, chunks[2][0] + chunks[2][1], *tail)
    got2 = send(made)
    made = project((chunk(3, 0),), att, residual, sel, chunks[3][0], *tail)
    got3 = send(made)
    made = project((chunk(3, 1),), att, residual, sel, chunks[3][1], *tail)
    got4 = send(made)

    early = tuple((step, 0, columns) for step in range(3))
    late = tuple((3, off, width) for off, width in zip(offs, splits))
    known = len(early) + 1
    first, logits = map(
        near,
        first_probe((early + late)[:known], residual, probes, label_row, hidden[:known], ring, columns),
    )
    cuts = second_probe(
        early + late, known, probes, label_row, first, logits, hidden, group, ring, columns
    )
    cuts = [near(c) for c in cuts]
    total = add_up([cuts[0]] + [swap(cuts[j], "dp", j) for j in range(1, group)])
    for j in (1, 2):
        total = add_up([total, swap(total, "shard", j)])
    grads = gradient([total] + [swap(total, "dp", j) for j in range(1, group)])

    where = (group, ring, columns)
    out = place(early, got0 + got1 + got2, None, shape, *where)
    out = place(late, got3 + got4, out, shape, *where)
    return out, jnp.swapaxes(grads, 1, 2)


def general_probe_kernel(tok_count, label_ref, probe_ref, chunk_ref, grad_ref):
    chunk = chunk_ref[...]
    logits = lax.dot_general(probe_ref[...], chunk, NT, preferred_element_type=F32)
    mismatch = mismatch_of(logits, label_ref[...], tok_count)
    grad_ref[...] = jnp.dot(mismatch, chunk, preferred_element_type=F32)


def general_probe(label_row, probe, represent):
    return pl.pallas_call(
        functools.partial(general_probe_kernel, label_row.shape[1]),
        in_specs=[VMEM] * 3,
        out_specs=VMEM,
        out_shape=jax.ShapeDtypeStruct(probe.shape, F32),
        name="probe",
    )(label_row, probe, represent)


def per_device_general(projected, residual, out_weight, probe_weight, labels, lengths, destination):
    group, ring = lax.axis_size("dp"), lax.axis_size("shard")
    me, z = lax.axis_index("dp"), lax.axis_index("shard")
    slot_count = -(-lengths.shape[1] // group)
    columns = out_weight.shape[1]
    hidden_width = residual.shape[1]
    att, sel = attention(projected, lengths[0], destination[0], group, slot_count)
    hidden = jnp.zeros(residual.shape, BF16)
    held = out_weight
    for step in range(ring):
        if step:
            held = lax.ppermute(held, "shard", [(i, (i + 1) % ring) for i in range(ring)])
        col = lax.rem(z + ring - step, ring) * columns
        resid = lax.dynamic_slice(residual, (0, col), (residual.shape[0], columns))
        mixed = jnp.dot(att, held, preferred_element_type=F32) + resid.astype(F32)
        hidden = lax.dynamic_update_slice(hidden, mixed.astype(BF16), (0, col))
    label_row = labels.reshape(1, -1)
    probes = jnp.swapaxes(probe_weight, 1, 2)
    grads = [general_probe(label_row, probes[k], r) for k, r in enumerate((residual, hidden))]
    grads = lax.psum(jnp.stack(grads), ("dp", "shard"))
    packed = jnp.dot(sel, hidden, preferred_element_type=F32).astype(BF16)
    packed = packed.reshape(group, slot_count * LMAX, hidden_width)
    places = jnp.arange(group, dtype=I32)
    spots = places ^ me if is_pow2(group) else lax.rem(places + group - me, group)
    packed = jnp.take(packed, spots, axis=0)
    packed = lax.all_to_all(packed, "dp", split_axis=0, concat_axis=0, tiled=True)
    return packed.reshape(-1, hidden_width), jnp.swapaxes(grads, 1, 2)


def solution(mesh):
    def per_device(projected, residual, out_weight, *rest):
        fast = is_fast(dict(mesh.shape), out_weight.shape[1], out_weight.shape[0])
        body = per_device_fast if fast else per_device_general
        return body(projected, residual, out_weight, *rest)

    return jax.shard_map(
        per_device,
        mesh=mesh,
        in_specs=(
            P(("parts", "dp", "shard"), None),
            P(("parts", "dp", "shard"), None),
            P(None, "shard"),
            P(),
            P(("parts", "dp", "shard")),
            P(("parts", "dp", "shard"), None),
            P(("parts", "dp", "shard"), None),
        ),
        out_specs=(P(("parts", "dp", "shard"), None), P("parts", None, None)),
        check_vma=False,
    )
```

time: 350 us -> 135 us (0.39)
  the two profiles are of different devices: /device:TPU:8 before, /device:TPU:0 now
where the time goes in v2:
time: 135 us; the launch traced here: 134 us
  waiting for transfers between devices  75.7 us (56%)
  starting transfers between devices  34.9 us (26%)
  Pallas kernels  20.8 us (15%)
  local copies, waits for them, and re-layouts  2.07 us (2%)
    ppermute x41, waiting for transfers between devices, swap(): return near(lax.ppermute(x, axis, pairs))  43.5 us
    ppermute x6, waiting for transfers between devices, rotate(): return near(lax.ppermute(x, axis, [(i, (i + 1) % n) for i in range(n)]))  32.3 us
    ppermute x41, starting transfers between devices, swap(): return near(lax.ppermute(x, axis, pairs))  27.4 us
    pallas_call x5, Pallas kernels, project(): pl.pallas_call(functools.partial(project_kernel, blocks, group, ring, cor...  8.69 us
    ppermute x6, starting transfers between devices, rotate(): return near(lax.ppermute(x, axis, [(i, (i + 1) % n) for i in range(n)]))  7.56 us
    pallas_call x1, Pallas kernels, attention(): pl.pallas_call(functools.partial(attention_kernel, lengths.shape[0], slot...  5.65 us
  transfers between devices with their start and end apart: 47, of which 19 were waited for; matrix products, arithmetic and copies ran while one was open for 0% of the time, Pallas kernels for 14%

profile of v2, /device:TPU:0, one launch (start us, length us, event | category | flops | bytes accessed | tf_op | source)
XLA Modules:
  0.0 134.4 jit_solution(5250138451614403894)
XLA Ops:
  1.9 3.1 %collective-permute-start = (bf16[640,384]{1,0:T(8,128)(2,1)S(1)}, bf16[640,384]{1,0:T(8,128)(2,1)S(1)}, u32[]{:S(2)}, u32[]{:S(2)}) collective-permute-start(bf16[640,384]{1,0:T(8,128)(2,1)S(1)} %get-tuple-element.39), channel_id=1, source_target_pairs={{0,1},{1,2},{2,3},{3,0},{4,5},{5,6},{6,7},{7,4},{8,9},{9,10},{10,1... | collective-permute-start | bytes 1474568 | tf_op jit(solution)/shard_map/ppermute | solution.py:138
  5.0 1.6 %collective-permute-start.9 = (bf16[640,256]{1,0:T(8,128)(2,1)S(1)}, bf16[640,256]{1,0:T(8,128)(2,1)S(1)}, u32[]{:S(2)}, u32[]{:S(2)}) collective-permute-start(bf16[640,256]{1,0:T(8,128)(2,1)S(1)} %get-tuple-element.44), channel_id=1, source_target_pairs={{0,1},{1,2},{2,3},{3,0},{4,5},{5,6},{6,7},{7,4},{8,9},{9,10},{10,1... | collective-permute-start | bytes 983048 | tf_op jit(solution)/shard_map/ppermute | solution.py:138
  6.6 18.7 %collective-permute-done.9.refs_4_ = bf16[640,256]{1,0:T(8,128)(2,1)S(1)} collective-permute-done((bf16[640,256]{1,0:T(8,128)(2,1)S(1)}, bf16[640,256]{1,0:T(8,128)(2,1)S(1)}, u32[]{:S(2)}, u32[]{:S(2)}) %collective-permute-start.9) | collective-permute-done | bytes 327712 | tf_op jit(solution)/shard_map/ppermute | solution.py:138
  25.3 1.3 collective-permute-start.1
  26.6 1.5 %collective-permute-start.24 = (bf16[640,256]{1,0:T(8,128)(2,1)S(1)}, bf16[640,256]{1,0:T(8,128)(2,1)S(1)}, u32[]{:S(2)}, u32[]{:S(2)}) collective-permute-start(bf16[640,256]{1,0:T(8,128)(2,1)S(1)} %collective-permute-done.9.refs_4_), channel_id=1, source_target_pairs={{0,16},{16,0},{1,17},{17,1},{2,18},{18,2},{3,19},{19,3},{4,20},{20... | collective-permute-start | bytes 983048 | tf_op jit(solution)/shard_map/ppermute | solution.py:133
  28.1 2.0 %copy-done.1 = bf16[240,7680]{1,0:T(8,128)(2,1)S(1)} copy-done((bf16[240,7680]{1,0:T(8,128)(2,1)S(1)}, bf16[240,7680]{1,0:T(8,128)(2,1)}, u32[]{:S(2)}) %copy-start.1) | copy-done | bytes 3686424
  30.1 5.6 %attention.1 = (bf16[240,2560]{1,0:T(8,128)(2,1)S(1)}, bf16[576,240]{1,0:T(8,128)(2,1)S(1)}) custom-call(s32[9]{0:T(128)S(1)} %bitcast.9, s32[9]{0:T(128)S(1)} %bitcast.10, bf16[240,7680]{1,0:T(8,128)(2,1)S(1)} %copy-done.1, bf16[240,7680]{1,0:T(8,128)(2,1)S(1)} %copy-done.1, bf16[240,7680]{1,0:T(8,128)(2,1)S(1)} %copy-done.1), custom_call_target="tpu_custom_call" | custom-call | tf_op jit(solution)/shard_map/attention/pallas_call | solution.py:111
  35.8 1.5 %project.7 = (bf16[144,640]{1,0:T(8,128)(2,1)S(1)}, bf16[144,640]{1,0:T(8,128)(2,1)S(1)}, bf16[144,640]{1,0:T(8,128)(2,1)S(1)}, bf16[144,640]{1,0:T(8,128)(2,1)S(1)}, bf16[240,640]{1,0:T(8,128)(2,1)S(1)}) custom-call(bf16[240,2560]{1,0:T(8,128)(2,1)S(1)} %get-tuple-element.37.att_ref, bf16[240,2560]{1,0:T(8,128)(2,1)S(1)} %copy-done, ...), custom_call_target="tpu_custom_call" | custom-call | tf_op jit(solution)/shard_map/project/pallas_call | solution.py:306
  37.8 1.3 collective-permute-start.33
  39.9 6.6 %collective-permute-done.1.refs_0_ = bf16[640,384]{1,0:T(8,128)(2,1)S(1)} collective-permute-done((bf16[640,384]{1,0:T(8,128)(2,1)S(1)}, bf16[640,384]{1,0:T(8,128)(2,1)S(1)}, u32[]{:S(2)}, u32[]{:S(2)}) %collective-permute-start.1) | collective-permute-done | bytes 491552 | tf_op jit(solution)/shard_map/ppermute | solution.py:138
  46.5 1.9 %collective-permute-done.33.refs_5_ = bf16[640,256]{1,0:T(8,128)(2,1)S(1)} collective-permute-done((bf16[640,256]{1,0:T(8,128)(2,1)S(1)}, bf16[640,256]{1,0:T(8,128)(2,1)S(1)}, u32[]{:S(2)}, u32[]{:S(2)}) %collective-permute-start.33) | collective-permute-done | bytes 327712 | tf_op jit(solution)/shard_map/ppermute | solution.py:133
  48.4 1.6 %collective-permute-start.11 = (bf16[640,256]{1,0:T(8,128)(2,1)S(1)}, bf16[640,256]{1,0:T(8,128)(2,1)S(1)}, u32[]{:S(2)}, u32[]{:S(2)}) collective-permute-start(bf16[640,256]{1,0:T(8,128)(2,1)S(1)} %collective-permute-done.10.refs_4_), channel_id=1, source_target_pairs={{0,1},{1,2},{2,3},{3,0},{4,5},{5,6},{6,7},{7,4},{8,9},{9,10},{10,1... | collective-permute-start | bytes 983048 | tf_op jit(solution)/shard_map/ppermute | solution.py:138
  50.0 8.1 %collective-permute-done.21.refs_1_ = bf16[640,384]{1,0:T(8,128)(2,1)S(1)} collective-permute-done((bf16[640,384]{1,0:T(8,128)(2,1)S(1)}, bf16[640,384]{1,0:T(8,128)(2,1)S(1)}, u32[]{:S(2)}, u32[]{:S(2)}) %collective-permute-start.21) | collective-permute-done | bytes 491552 | tf_op jit(solution)/shard_map/ppermute | solution.py:133
  58.6 3.8 %collective-permute-done.2.refs_0_ = bf16[640,384]{1,0:T(8,128)(2,1)S(1)} collective-permute-done((bf16[640,384]{1,0:T(8,128)(2,1)S(1)}, bf16[640,384]{1,0:T(8,128)(2,1)S(1)}, u32[]{:S(2)}, u32[]{:S(2)}) %collective-permute-start.2) | collective-permute-done | bytes 491552 | tf_op jit(solution)/shard_map/ppermute | solution.py:138
  62.4 1.3 collective-permute-start.3
  63.6 3.2 %collective-permute-done.11.refs_0_ = bf16[640,256]{1,0:T(8,128)(2,1)S(1)} collective-permute-done((bf16[640,256]{1,0:T(8,128)(2,1)S(1)}, bf16[640,256]{1,0:T(8,128)(2,1)S(1)}, u32[]{:S(2)}, u32[]{:S(2)}) %collective-permute-start.11) | collective-permute-done | bytes 327712 | tf_op jit(solution)/shard_map/ppermute | solution.py:138
  68.4 20.9 %collective-permute-done.12.refs_1_ = bf16[640,256]{1,0:T(8,128)(2,1)S(1)} collective-permute-done((bf16[640,256]{1,0:T(8,128)(2,1)S(1)}, bf16[640,256]{1,0:T(8,128)(2,1)S(1)}, u32[]{:S(2)}, u32[]{:S(2)}) %collective-permute-start.12) | collective-permute-done | bytes 327712 | tf_op jit(solution)/shard_map/ppermute | solution.py:133
  91.1 1.5 %collective-permute-start.19 = (bf16[144,640]{1,0:T(8,128)(2,1)S(1)}, bf16[144,640]{1,0:T(8,128)(2,1)S(1)}, u32[]{:S(2)}, u32[]{:S(2)}) collective-permute-start(bf16[144,640]{1,0:T(8,128)(2,1)S(1)} %get-tuple-element.51), channel_id=1, source_target_pairs={{0,8},{4,12},{8,0},{12,4},{1,9},{5,13},{9,1},{13,5},{2,10},{6,14},... | collective-permute-start | bytes 552968 | tf_op jit(solution)/shard_map/ppermute | solution.py:133
  95.0 2.5 %project.8 = (bf16[144,640]{1,0:T(8,128)(2,1)S(1)}, bf16[144,640]{1,0:T(8,128)(2,1)S(1)}, bf16[144,640]{1,0:T(8,128)(2,1)S(1)}, bf16[144,640]{1,0:T(8,128)(2,1)S(1)}, bf16[240,640]{1,0:T(8,128)(2,1)S(1)}) custom-call(bf16[240,2560]{1,0:T(8,128)(2,1)S(1)} %get-tuple-element.37.att_ref, bf16[240,2560]{1,0:T(8,128)(2,1)S(1)} %copy-done, ...), custom_call_target="tpu_custom_call" | custom-call | tf_op jit(solution)/shard_map/project/pallas_call | solution.py:306
  100.4 2.6 %project.9 = (bf16[144,640]{1,0:T(8,128)(2,1)S(1)}, bf16[144,640]{1,0:T(8,128)(2,1)S(1)}, bf16[144,640]{1,0:T(8,128)(2,1)S(1)}, bf16[144,640]{1,0:T(8,128)(2,1)S(1)}, bf16[240,640]{1,0:T(8,128)(2,1)S(1)}) custom-call(bf16[240,2560]{1,0:T(8,128)(2,1)S(1)} %get-tuple-element.37.att_ref, bf16[240,2560]{1,0:T(8,128)(2,1)S(1)} %copy-done, ...), custom_call_target="tpu_custom_call" | custom-call | tf_op jit(solution)/shard_map/project/pallas_call | solution.py:306
  104.2 1.7 %first_probe.1 = (f32[8,2560]{1,0:T(8,128)S(1)}, f32[8,240]{1,0:T(8,128)S(1)}) custom-call(bf16[240,2560]{1,0:T(8,128)(2,1)S(1)} %copy-done, bf16[2,8,2560]{2,1,0:T(8,128)(2,1)S(1)} %bitcast.5, s32[1,240]{1,0:T(1,128)S(1)} %bitcast.7, bf16[240,640]{1,0:T(8,128)(2,1)S(1)} %get-tuple-element.61.refs_0_, bf16[240,640]{1,0:T(8,128)(2,1)S(1)} %get-tuple-element.62.refs_1_, ...), custom_call_target="tpu_custom_call" | custom-call | tf_op jit(solution)/shard_map/first_probe/pallas_call | solution.py:221
  108.6 2.7 %collective-permute-done.40.refs_2_ = f32[16,640]{1,0:T(8,128)S(1)} collective-permute-done((f32[16,640]{1,0:T(8,128)S(1)}, f32[16,640]{1,0:T(8,128)S(1)}, u32[]{:S(2)}, u32[]{:S(2)}) %collective-permute-start.40) | collective-permute-done | bytes 40992 | tf_op jit(solution)/shard_map/ppermute | solution.py:133
  111.9 1.6 %collective-permute-start.42 = (f32[16,640]{1,0:T(8,128)S(1)}, f32[16,640]{1,0:T(8,128)S(1)}, u32[]{:S(2)}, u32[]{:S(2)}) collective-permute-start(f32[16,640]{1,0:T(8,128)S(1)} %add_up.3.refs_0_), channel_id=1, source_target_pairs={{0,1},{1,0},{2,3},{3,2},{4,5},{5,4},{6,7},{7,6},{8,9},{9,8},{10,11... | collective-permute-start | bytes 122888 | tf_op jit(solution)/shard_map/ppermute | solution.py:133
  113.5 1.3 collective-permute-start.16
  114.9 1.4 %collective-permute-start.37 = (bf16[144,640]{1,0:T(8,128)(2,1)S(1)}, bf16[144,640]{1,0:T(8,128)(2,1)S(1)}, u32[]{:S(2)}, u32[]{:S(2)}) collective-permute-start(bf16[144,640]{1,0:T(8,128)(2,1)S(1)} %get-tuple-element.59), channel_id=1, source_target_pairs={{0,8},{4,12},{8,0},{12,4},{1,9},{5,13},{9,1},{13,5},{2,10},{6,14},... | collective-permute-start | bytes 552968 | tf_op jit(solution)/shard_map/ppermute | solution.py:133
  117.9 1.9 %collective-permute-start.43 = (f32[16,640]{1,0:T(8,128)S(1)}, f32[16,640]{1,0:T(8,128)S(1)}, u32[]{:S(2)}, u32[]{:S(2)}) collective-permute-start(f32[16,640]{1,0:T(8,128)S(1)} %add_up.4.refs_0_), channel_id=1, source_target_pairs={{0,2},{1,3},{2,0},{3,1},{4,6},{5,7},{6,4},{7,5},{8,10},{9,11},{10,... | collective-permute-start | bytes 122888 | tf_op jit(solution)/shard_map/ppermute | solution.py:133
  120.2 1.4 %collective-permute-start.7 = (bf16[144,384]{1,0:T(8,128)(2,1)S(1)}, bf16[144,384]{1,0:T(8,128)(2,1)S(1)}, u32[]{:S(2)}, u32[]{:S(2)}) collective-permute-start(bf16[144,384]{1,0:T(8,128)(2,1)S(1)} %get-tuple-element.42), channel_id=1, source_target_pairs={{0,8},{4,12},{8,0},{12,4},{1,9},{5,13},{9,1},{13,5},{2,10},{6,14},... | collective-permute-start | bytes 331784 | tf_op jit(solution)/shard_map/ppermute | solution.py:133
  121.6 1.7 %collective-permute-done.43.refs_1_ = f32[16,640]{1,0:T(8,128)S(1)} collective-permute-done((f32[16,640]{1,0:T(8,128)S(1)}, f32[16,640]{1,0:T(8,128)S(1)}, u32[]{:S(2)}, u32[]{:S(2)}) %collective-permute-start.43) | collective-permute-done | bytes 40992 | tf_op jit(solution)/shard_map/ppermute | solution.py:133
  123.5 1.8 %collective-permute-start.44 = (f32[16,640]{1,0:T(8,128)S(1)}, f32[16,640]{1,0:T(8,128)S(1)}, u32[]{:S(2)}, u32[]{:S(2)}) collective-permute-start(f32[16,640]{1,0:T(8,128)S(1)} %add_up.5.refs_0_), channel_id=1, source_target_pairs={{0,4},{4,0},{8,12},{12,8},{1,5},{5,1},{9,13},{13,9},{2,6},{6,2},{1... | collective-permute-start | bytes 122888 | tf_op jit(solution)/shard_map/ppermute | solution.py:133
  125.3 2.0 %collective-permute-done.38.refs_11_ = bf16[144,640]{1,0:T(8,128)(2,1)S(1)} collective-permute-done((bf16[144,640]{1,0:T(8,128)(2,1)S(1)}, bf16[144,640]{1,0:T(8,128)(2,1)S(1)}, u32[]{:S(2)}, u32[]{:S(2)}) %collective-permute-start.38) | collective-permute-done | bytes 184352 | tf_op jit(solution)/shard_map/ppermute | solution.py:133
  128.7 1.4 %place.2.refs_8_ = bf16[576,2560]{1,0:T(8,128)(2,1)} custom-call(bf16[144,640]{1,0:T(8,128)(2,1)S(1)} %get-tuple-element.49.refs_0_, bf16[144,640]{1,0:T(8,128)(2,1)S(1)} %collective-permute-done.18.refs_1_, bf16[144,640]{1,0:T(8,128)(2,1)S(1)} %collective-permute-done.19.refs_2_, bf16[144,640]{1,0:T(8,128)(2,1)S(1)} %collective-permute-done.20.refs_3_, ...), custom_call_target="tpu_custom_call" | custom-call | tf_op jit(solution)/shard_map/place/pallas_call | solution.py:342
  130.2 1.8 %collective-permute-done.8.refs_3_ = bf16[144,384]{1,0:T(8,128)(2,1)S(1)} collective-permute-done((bf16[144,384]{1,0:T(8,128)(2,1)S(1)}, bf16[144,384]{1,0:T(8,128)(2,1)S(1)}, u32[]{:S(2)}, u32[]{:S(2)}) %collective-permute-start.8) | collective-permute-done | bytes 110624 | tf_op jit(solution)/shard_map/ppermute | solution.py:133
  (91 shorter events, 22.5 us)
Async XLA Ops:
  1.9 23.4 %collective-permute-start = (bf16[640,384]{1,0:T(8,128)(2,1)S(1)}, bf16[640,384]{1,0:T(8,128)(2,1)S(1)}, u32[]{:S(2)}, u32[]{:S(2)}) collective-permute-start(bf16[640,384]{1,0:T(8,128)(2,1)S(1)} %get-tuple-element.39), channel_id=1, source_target_pairs={{0,1},{1,2},{2,3},{3,0},{4,5},{5,6},{6,7},{7,4},{8,9},{9,10},{10,1... | collective-permute-start | bytes 1474568 | tf_op jit(solution)/shard_map/ppermute | solution.py:138
  5.0 20.3 %collective-permute-start.9 = (bf16[640,256]{1,0:T(8,128)(2,1)S(1)}, bf16[640,256]{1,0:T(8,128)(2,1)S(1)}, u32[]{:S(2)}, u32[]{:S(2)}) collective-permute-start(bf16[640,256]{1,0:T(8,128)(2,1)S(1)} %get-tuple-element.44), channel_id=1, source_target_pairs={{0,1},{1,2},{2,3},{3,0},{4,5},{5,6},{6,7},{7,4},{8,9},{9,10},{10,1... | collective-permute-start | bytes 983048 | tf_op jit(solution)/shard_map/ppermute | solution.py:138
  25.3 12.6 %collective-permute-start.10 = (bf16[640,256]{1,0:T(8,128)(2,1)S(1)}, bf16[640,256]{1,0:T(8,128)(2,1)S(1)}, u32[]{:S(2)}, u32[]{:S(2)}) collective-permute-start(bf16[640,256]{1,0:T(8,128)(2,1)S(1)} %collective-permute-done.9.refs_4_), channel_id=1, source_target_pairs={{0,1},{1,2},{2,3},{3,0},{4,5},{5,6},{6,7},{7,4},{8,9},{9,10},{10,1... | collective-permute-start | bytes 983048 | tf_op jit(solution)/shard_map/ppermute | solution.py:138
  25.3 21.2 %collective-permute-start.1 = (bf16[640,384]{1,0:T(8,128)(2,1)S(1)}, bf16[640,384]{1,0:T(8,128)(2,1)S(1)}, u32[]{:S(2)}, u32[]{:S(2)}) collective-permute-start(bf16[640,384]{1,0:T(8,128)(2,1)S(1)} %collective-permute-done.refs_0_), channel_id=1, source_target_pairs={{0,1},{1,2},{2,3},{3,0},{4,5},{5,6},{6,7},{7,4},{8,9},{9,10},{10,1... | collective-permute-start | bytes 1474568 | tf_op jit(solution)/shard_map/ppermute | solution.py:138
  26.6 13.3 %collective-permute-start.24 = (bf16[640,256]{1,0:T(8,128)(2,1)S(1)}, bf16[640,256]{1,0:T(8,128)(2,1)S(1)}, u32[]{:S(2)}, u32[]{:S(2)}) collective-permute-start(bf16[640,256]{1,0:T(8,128)(2,1)S(1)} %collective-permute-done.9.refs_4_), channel_id=1, source_target_pairs={{0,16},{16,0},{1,17},{17,1},{2,18},{18,2},{3,19},{19,3},{4,20},{20... | collective-permute-start | bytes 983048 | tf_op jit(solution)/shard_map/ppermute | solution.py:133
  37.3 9.2 %collective-permute-start.25 = (bf16[640,256]{1,0:T(8,128)(2,1)S(1)}, bf16[640,256]{1,0:T(8,128)(2,1)S(1)}, u32[]{:S(2)}, u32[]{:S(2)}) collective-permute-start(bf16[640,256]{1,0:T(8,128)(2,1)S(1)} %collective-permute-done.9.refs_4_), channel_id=1, source_target_pairs={{0,4},{4,0},{8,12},{12,8},{1,5},{5,1},{9,13},{13,9},{2,6},{6,2},{1... | collective-permute-start | bytes 983048 | tf_op jit(solution)/shard_map/ppermute | solution.py:133
  37.8 10.6 %collective-permute-start.33 = (bf16[640,256]{1,0:T(8,128)(2,1)S(1)}, bf16[640,256]{1,0:T(8,128)(2,1)S(1)}, u32[]{:S(2)}, u32[]{:S(2)}) collective-permute-start(bf16[640,256]{1,0:T(8,128)(2,1)S(1)} %collective-permute-done.10.refs_4_), channel_id=1, source_target_pairs={{0,16},{16,0},{1,17},{17,1},{2,18},{18,2},{3,19},{19,3},{4,20},{20... | collective-permute-start | bytes 983048 | tf_op jit(solution)/shard_map/ppermute | solution.py:133
  39.1 18.9 %collective-permute-start.21 = (bf16[640,384]{1,0:T(8,128)(2,1)S(1)}, bf16[640,384]{1,0:T(8,128)(2,1)S(1)}, u32[]{:S(2)}, u32[]{:S(2)}) collective-permute-start(bf16[640,384]{1,0:T(8,128)(2,1)S(1)} %collective-permute-done.refs_0_), channel_id=1, source_target_pairs={{0,16},{16,0},{1,17},{17,1},{2,18},{18,2},{3,19},{19,3},{4,20},{20... | collective-permute-start | bytes 1474568 | tf_op jit(solution)/shard_map/ppermute | solution.py:133
  39.9 8.6 %collective-permute-start.34 = (bf16[640,256]{1,0:T(8,128)(2,1)S(1)}, bf16[640,256]{1,0:T(8,128)(2,1)S(1)}, u32[]{:S(2)}, u32[]{:S(2)}) collective-permute-start(bf16[640,256]{1,0:T(8,128)(2,1)S(1)} %collective-permute-done.10.refs_4_), channel_id=1, source_target_pairs={{0,4},{4,0},{8,12},{12,8},{1,5},{5,1},{9,13},{13,9},{2,6},{6,2},{1... | collective-permute-start | bytes 983048 | tf_op jit(solution)/shard_map/ppermute | solution.py:133
  46.5 15.9 %collective-permute-start.2 = (bf16[640,384]{1,0:T(8,128)(2,1)S(1)}, bf16[640,384]{1,0:T(8,128)(2,1)S(1)}, u32[]{:S(2)}, u32[]{:S(2)}) collective-permute-start(bf16[640,384]{1,0:T(8,128)(2,1)S(1)} %collective-permute-done.1.refs_0_), channel_id=1, source_target_pairs={{0,1},{1,2},{2,3},{3,0},{4,5},{5,6},{6,7},{7,4},{8,9},{9,10},{10,1... | collective-permute-start | bytes 1474568 | tf_op jit(solution)/shard_map/ppermute | solution.py:138
  46.5 21.4 %collective-permute-start.22 = (bf16[640,384]{1,0:T(8,128)(2,1)S(1)}, bf16[640,384]{1,0:T(8,128)(2,1)S(1)}, u32[]{:S(2)}, u32[]{:S(2)}) collective-permute-start(bf16[640,384]{1,0:T(8,128)(2,1)S(1)} %collective-permute-done.refs_0_), channel_id=1, source_target_pairs={{0,4},{4,0},{8,12},{12,8},{1,5},{5,1},{9,13},{13,9},{2,6},{6,2},{1... | collective-permute-start | bytes 1474568 | tf_op jit(solution)/shard_map/ppermute | solution.py:133
  48.4 9.7 %collective-permute-start.26 = (bf16[640,256]{1,0:T(8,128)(2,1)S(1)}, bf16[640,256]{1,0:T(8,128)(2,1)S(1)}, u32[]{:S(2)}, u32[]{:S(2)}) collective-permute-start(bf16[640,256]{1,0:T(8,128)(2,1)S(1)} %collective-permute-done.24.refs_5_), channel_id=1, source_target_pairs={{0,4},{4,0},{8,12},{12,8},{1,5},{5,1},{9,13},{13,9},{2,6},{6,2},{1... | collective-permute-start | bytes 983048 | tf_op jit(solution)/shard_map/ppermute | solution.py:133
  48.4 18.4 %collective-permute-start.11 = (bf16[640,256]{1,0:T(8,128)(2,1)S(1)}, bf16[640,256]{1,0:T(8,128)(2,1)S(1)}, u32[]{:S(2)}, u32[]{:S(2)}) collective-permute-start(bf16[640,256]{1,0:T(8,128)(2,1)S(1)} %collective-permute-done.10.refs_4_), channel_id=1, source_target_pairs={{0,1},{1,2},{2,3},{3,0},{4,5},{5,6},{6,7},{7,4},{8,9},{9,10},{10,1... | collective-permute-start | bytes 983048 | tf_op jit(solution)/shard_map/ppermute | solution.py:138
  58.1 9.8 %collective-permute-start.35 = (bf16[640,256]{1,0:T(8,128)(2,1)S(1)}, bf16[640,256]{1,0:T(8,128)(2,1)S(1)}, u32[]{:S(2)}, u32[]{:S(2)}) collective-permute-start(bf16[640,256]{1,0:T(8,128)(2,1)S(1)} %collective-permute-done.33.refs_5_), channel_id=1, source_target_pairs={{0,4},{4,0},{8,12},{12,8},{1,5},{5,1},{9,13},{13,9},{2,6},{6,2},{1... | collective-permute-start | bytes 983048 | tf_op jit(solution)/shard_map/ppermute | solution.py:133
  58.1 31.2 %collective-permute-start.30 = (bf16[640,384]{1,0:T(8,128)(2,1)S(1)}, bf16[640,384]{1,0:T(8,128)(2,1)S(1)}, u32[]{:S(2)}, u32[]{:S(2)}) collective-permute-start(bf16[640,384]{1,0:T(8,128)(2,1)S(1)} %collective-permute-done.1.refs_0_), channel_id=1, source_target_pairs={{0,16},{16,0},{1,17},{17,1},{2,18},{18,2},{3,19},{19,3},{4,20},{20... | collective-permute-start | bytes 1474568 | tf_op jit(solution)/shard_map/ppermute | solution.py:133
  62.4 27.5 %collective-permute-start.3 = (bf16[640,384]{1,0:T(8,128)(2,1)S(1)}, bf16[640,384]{1,0:T(8,128)(2,1)S(1)}, u32[]{:S(2)}, u32[]{:S(2)}) collective-permute-start(bf16[640,384]{1,0:T(8,128)(2,1)S(1)} %collective-permute-done.2.refs_0_), channel_id=1, source_target_pairs={{0,16},{16,0},{1,17},{17,1},{2,18},{18,2},{3,19},{19,3},{4,20},{20... | collective-permute-start | bytes 1474568 | tf_op jit(solution)/shard_map/ppermute | solution.py:133
  66.8 22.4 %collective-permute-start.12 = (bf16[640,256]{1,0:T(8,128)(2,1)S(1)}, bf16[640,256]{1,0:T(8,128)(2,1)S(1)}, u32[]{:S(2)}, u32[]{:S(2)}) collective-permute-start(bf16[640,256]{1,0:T(8,128)(2,1)S(1)} %collective-permute-done.11.refs_0_), channel_id=1, source_target_pairs={{0,16},{16,0},{1,17},{17,1},{2,18},{18,2},{3,19},{19,3},{4,20},{20... | collective-permute-start | bytes 983048 | tf_op jit(solution)/shard_map/ppermute | solution.py:133
  67.9 22.4 %collective-permute-start.31 = (bf16[640,384]{1,0:T(8,128)(2,1)S(1)}, bf16[640,384]{1,0:T(8,128)(2,1)S(1)}, u32[]{:S(2)}, u32[]{:S(2)}) collective-permute-start(bf16[640,384]{1,0:T(8,128)(2,1)S(1)} %collective-permute-done.1.refs_0_), channel_id=1, source_target_pairs={{0,4},{4,0},{8,12},{12,8},{1,5},{5,1},{9,13},{13,9},{2,6},{6,2},{1... | collective-permute-start | bytes 1474568 | tf_op jit(solution)/shard_map/ppermute | solution.py:133
  67.9 21.9 %collective-permute-start.13 = (bf16[640,256]{1,0:T(8,128)(2,1)S(1)}, bf16[640,256]{1,0:T(8,128)(2,1)S(1)}, u32[]{:S(2)}, u32[]{:S(2)}) collective-permute-start(bf16[640,256]{1,0:T(8,128)(2,1)S(1)} %collective-permute-done.11.refs_0_), channel_id=1, source_target_pairs={{0,4},{4,0},{8,12},{12,8},{1,5},{5,1},{9,13},{13,9},{2,6},{6,2},{1... | collective-permute-start | bytes 983048 | tf_op jit(solution)/shard_map/ppermute | solution.py:133
  89.3 8.3 %collective-permute-start.32 = (bf16[640,384]{1,0:T(8,128)(2,1)S(1)}, bf16[640,384]{1,0:T(8,128)(2,1)S(1)}, u32[]{:S(2)}, u32[]{:S(2)}) collective-permute-start(bf16[640,384]{1,0:T(8,128)(2,1)S(1)} %collective-permute-done.30.refs_1_), channel_id=1, source_target_pairs={{0,4},{4,0},{8,12},{12,8},{1,5},{5,1},{9,13},{13,9},{2,6},{6,2},{1... | collective-permute-start | bytes 1474568 | tf_op jit(solution)/shard_map/ppermute | solution.py:133
  89.8 8.6 %collective-permute-start.5 = (bf16[640,384]{1,0:T(8,128)(2,1)S(1)}, bf16[640,384]{1,0:T(8,128)(2,1)S(1)}, u32[]{:S(2)}, u32[]{:S(2)}) collective-permute-start(bf16[640,384]{1,0:T(8,128)(2,1)S(1)} %collective-permute-done.3.refs_1_), channel_id=1, source_target_pairs={{0,4},{4,0},{8,12},{12,8},{1,5},{5,1},{9,13},{13,9},{2,6},{6,2},{1... | collective-permute-start | bytes 1474568 | tf_op jit(solution)/shard_map/ppermute | solution.py:133
  91.1 15.3 %collective-permute-start.19 = (bf16[144,640]{1,0:T(8,128)(2,1)S(1)}, bf16[144,640]{1,0:T(8,128)(2,1)S(1)}, u32[]{:S(2)}, u32[]{:S(2)}) collective-permute-start(bf16[144,640]{1,0:T(8,128)(2,1)S(1)} %get-tuple-element.51), channel_id=1, source_target_pairs={{0,8},{4,12},{8,0},{12,4},{1,9},{5,13},{9,1},{13,5},{2,10},{6,14},... | collective-permute-start | bytes 552968 | tf_op jit(solution)/shard_map/ppermute | solution.py:133
  93.7 13.4 %collective-permute-start.20 = (bf16[144,640]{1,0:T(8,128)(2,1)S(1)}, bf16[144,640]{1,0:T(8,128)(2,1)S(1)}, u32[]{:S(2)}, u32[]{:S(2)}) collective-permute-start(bf16[144,640]{1,0:T(8,128)(2,1)S(1)} %get-tuple-element.52), channel_id=1, source_target_pairs={{0,12},{4,8},{8,4},{12,0},{1,13},{5,9},{9,5},{13,1},{2,14},{6,10},... | collective-permute-start | bytes 552968 | tf_op jit(solution)/shard_map/ppermute | solution.py:133
  97.5 14.3 %collective-permute-start.27 = (bf16[144,640]{1,0:T(8,128)(2,1)S(1)}, bf16[144,640]{1,0:T(8,128)(2,1)S(1)}, u32[]{:S(2)}, u32[]{:S(2)}) collective-permute-start(bf16[144,640]{1,0:T(8,128)(2,1)S(1)} %get-tuple-element.54), channel_id=1, source_target_pairs={{0,4},{4,0},{8,12},{12,8},{1,5},{5,1},{9,13},{13,9},{2,6},{6,2},{1... | collective-permute-start | bytes 552968 | tf_op jit(solution)/shard_map/ppermute | solution.py:133
  98.0 15.6 %collective-permute-start.28 = (bf16[144,640]{1,0:T(8,128)(2,1)S(1)}, bf16[144,640]{1,0:T(8,128)(2,1)S(1)}, u32[]{:S(2)}, u32[]{:S(2)}) collective-permute-start(bf16[144,640]{1,0:T(8,128)(2,1)S(1)} %get-tuple-element.55), channel_id=1, source_target_pairs={{0,8},{4,12},{8,0},{12,4},{1,9},{5,13},{9,1},{13,5},{2,10},{6,14},... | collective-permute-start | bytes 552968 | tf_op jit(solution)/shard_map/ppermute | solution.py:133
  98.5 16.3 %collective-permute-start.29 = (bf16[144,640]{1,0:T(8,128)(2,1)S(1)}, bf16[144,640]{1,0:T(8,128)(2,1)S(1)}, u32[]{:S(2)}, u32[]{:S(2)}) collective-permute-start(bf16[144,640]{1,0:T(8,128)(2,1)S(1)} %get-tuple-element.56), channel_id=1, source_target_pairs={{0,12},{4,8},{8,4},{12,0},{1,13},{5,9},{9,5},{13,1},{2,14},{6,10},... | collective-permute-start | bytes 552968 | tf_op jit(solution)/shard_map/ppermute | solution.py:133
  111.6 8.6 %collective-permute-start.36 = (bf16[144,640]{1,0:T(8,128)(2,1)S(1)}, bf16[144,640]{1,0:T(8,128)(2,1)S(1)}, u32[]{:S(2)}, u32[]{:S(2)}) collective-permute-start(bf16[144,640]{1,0:T(8,128)(2,1)S(1)} %get-tuple-element.58), channel_id=1, source_target_pairs={{0,4},{4,0},{8,12},{12,8},{1,5},{5,1},{9,13},{13,9},{2,6},{6,2},{1... | collective-permute-start | bytes 552968 | tf_op jit(solution)/shard_map/ppermute | solution.py:133
  114.9 8.6 %collective-permute-start.37 = (bf16[144,640]{1,0:T(8,128)(2,1)S(1)}, bf16[144,640]{1,0:T(8,128)(2,1)S(1)}, u32[]{:S(2)}, u32[]{:S(2)}) collective-permute-start(bf16[144,640]{1,0:T(8,128)(2,1)S(1)} %get-tuple-element.59), channel_id=1, source_target_pairs={{0,8},{4,12},{8,0},{12,4},{1,9},{5,13},{9,1},{13,5},{2,10},{6,14},... | collective-permute-start | bytes 552968 | tf_op jit(solution)/shard_map/ppermute | solution.py:133
  116.3 11.0 %collective-permute-start.38 = (bf16[144,640]{1,0:T(8,128)(2,1)S(1)}, bf16[144,640]{1,0:T(8,128)(2,1)S(1)}, u32[]{:S(2)}, u32[]{:S(2)}) collective-permute-start(bf16[144,640]{1,0:T(8,128)(2,1)S(1)} %get-tuple-element.60), channel_id=1, source_target_pairs={{0,12},{4,8},{8,4},{12,0},{1,13},{5,9},{9,5},{13,1},{2,14},{6,10},... | collective-permute-start | bytes 552968 | tf_op jit(solution)/shard_map/ppermute | solution.py:133
  120.2 9.9 %collective-permute-start.7 = (bf16[144,384]{1,0:T(8,128)(2,1)S(1)}, bf16[144,384]{1,0:T(8,128)(2,1)S(1)}, u32[]{:S(2)}, u32[]{:S(2)}) collective-permute-start(bf16[144,384]{1,0:T(8,128)(2,1)S(1)} %get-tuple-element.42), channel_id=1, source_target_pairs={{0,8},{4,12},{8,0},{12,4},{1,9},{5,13},{9,1},{13,5},{2,10},{6,14},... | collective-permute-start | bytes 331784 | tf_op jit(solution)/shard_map/ppermute | solution.py:133
  123.3 8.7 %collective-permute-start.8 = (bf16[144,384]{1,0:T(8,128)(2,1)S(1)}, bf16[144,384]{1,0:T(8,128)(2,1)S(1)}, u32[]{:S(2)}, u32[]{:S(2)}) collective-permute-start(bf16[144,384]{1,0:T(8,128)(2,1)S(1)} %get-tuple-element.43), channel_id=1, source_target_pairs={{0,12},{4,8},{8,4},{12,0},{1,13},{5,9},{9,5},{13,1},{2,14},{6,10},... | collective-permute-start | bytes 331784 | tf_op jit(solution)/shard_map/ppermute | solution.py:133
  123.5 9.5 %collective-permute-start.44 = (f32[16,640]{1,0:T(8,128)S(1)}, f32[16,640]{1,0:T(8,128)S(1)}, u32[]{:S(2)}, u32[]{:S(2)}) collective-permute-start(f32[16,640]{1,0:T(8,128)S(1)} %add_up.5.refs_0_), channel_id=1, source_target_pairs={{0,4},{4,0},{8,12},{12,8},{1,5},{5,1},{9,13},{13,9},{2,6},{6,2},{1... | collective-permute-start | bytes 122888 | tf_op jit(solution)/shard_map/ppermute | solution.py:133
  (22 other events, 138.0 us)
